TPU v7x, 128 devices: a whole 4x4x4 slice. The times are simulated.
128 devices in a mesh: section: 2 (over core), row: 16 (over z, y), col: 4 (over x).
Axes of the slice: x: 4, y: 4, z: 4, core: 2. Of those that a mesh axis runs over, the one named last changes fastest.
Arguments:
- queries: bfloat16 [16384, 4096], P(('section', 'col'), 'row'), may hold values from -8 to 8
- keys: bfloat16 [16384, 512], P(('section', 'col')), may hold values from -6 to 6
- values: bfloat16 [16384, 512], P(('section', 'col')), may hold values from -6 to 6
- out_grad: bfloat16 [16384, 4096], P(('section', 'col'), 'row'), may hold values from -12 to 12
- q_weight: bfloat16 [2048, 4096], P('col', 'row'), may hold values from -0.125 to 0.125
- k_weight: bfloat16 [2048, 512], P('col'), may hold values from -0.125 to 0.125
- v_weight: bfloat16 [2048, 512], P('col'), may hold values from -0.125 to 0.125
- resid_grad: bfloat16 [16384, 2048], P(('section', 'row', 'col')), may hold values from -4 to 4
- moe_input: bfloat16 [16384, 2048], P(('section', 'row', 'col')), may hold values from -6 to 6
- expert_ids: int32 [16384, 8], P(('section', 'row', 'col')), may hold values from 0 to 127, all different within a row; in each aligned block of 128 rows (0 to 127, 128 to 255, ...) at most 9 rows name the same one
- route_weights: float32 [16384, 8], P(('section', 'row', 'col')), may hold values from 0.03 to 0.4
- w_gate_up: bfloat16 [128, 2048, 1536], P(('section', 'row', 'col')), may hold values from -0.125 to 0.125
- w_down: bfloat16 [128, 768, 2048], P(('section', 'row', 'col')), may hold values from -0.21875 to 0.21875
Outputs:
- moe_input_grad: bfloat16 [16384, 2048], P(('section', 'row', 'col'))
Inputs may be any that keep to these rules, and one draw needn't show every extreme that they name: `expert_ids`: each row names 8 different experts; among the rows of one device no expert is named by more than 9 rows, and in every draw some expert is named by exactly 9 rows of some device.
All inputs are finite; a program needn't handle non-finite values.
Results may differ from a plain program's by a relative error of at most 0.02.
Values may be sent and summed in bfloat16 or wider, within the bound.
No kernel may reach another device: no remote copies, remote signals or barrier semaphores. Data moves between devices by JAX's collectives and lax.ppermute only.
A program may use at most 128 MiB of HBM per device.

v0:
```python
from functools import partial

import jax
import jax.numpy as jnp
from jax import lax
from jax.sharding import PartitionSpec as P

HEADS = 32
KV_HEADS = 4
HEAD_DIM = 128
TOPK = 8
DOC = 1024


def split_up(shard, dim, length):
    lengths = shard.shape
    blocks = shard.reshape(*lengths[:dim], length, lengths[dim] // length, *lengths[dim + 1 :])
    return jnp.moveaxis(blocks, dim, 0)


def piece_ends(length, count):
    unit = 8 if length >= 8 * count else 1
    return [length // unit * k // count * unit for k in range(1, count)]


def joined_along(blocks, dim):
    blocks = jnp.moveaxis(blocks, 0, dim)
    lengths = blocks.shape
    return blocks.reshape(*lengths[:dim], lengths[dim] * lengths[dim + 1], *lengths[dim + 2 :])


def cut_exchange(shard, axis, pieces, split_dim, concat_dim):
    blocks = split_up(shard, split_dim, lax.axis_size(axis))
    widest = max(range(1, max(2, blocks.ndim - 1)), key=lambda d: blocks.shape[d])
    outs = []
    for piece in jnp.split(blocks, piece_ends(blocks.shape[widest], pieces), axis=widest):
        if piece.size:
            outs.append(lax.all_to_all(piece, axis, split_axis=0, concat_axis=0, tiled=True))
    return joined_along(jnp.concatenate(outs, axis=widest), concat_dim)


def items_in_groups(shard, axis, split_dim, concat_dim, work, item_dim, out_dim):
    items = jax.tree.leaves(shard)[0].shape[item_dim]
    count = 2 if items % 2 == 0 else 1
    outs = []
    for k in range(count):
        group = jax.tree.map(
            lambda a: lax.slice_in_dim(
                a, k * (items // count), (k + 1) * (items // count), axis=item_dim
            ),
            shard,
        )
        outs.append(
            work(
                lax.all_to_all(
                    group, axis, split_axis=split_dim, concat_axis=concat_dim, tiled=True
                )
            )
        )
    return jax.tree.map(lambda *parts: jnp.concatenate(parts, axis=out_dim), *outs)


def expert_math(rows_in, grad_in, w_gu, w_dn):
    width = w_dn.shape[0]
    gate_up = jnp.dot(rows_in, w_gu, preferred_element_type=jnp.float32)
    gate = gate_up[:, :width]
    up_part = gate_up[:, width:]
    dhidden = lax.dot_general(
        grad_in, w_dn, (((1,), (1,)), ((), ())), preferred_element_type=jnp.float32
    )
    sigm = jax.nn.sigmoid(gate)
    d_gate = dhidden * up_part * sigm * (1.0 + gate * (1.0 - sigm))
    d_up = dhidden * gate * sigm
    dgate_up = jnp.concatenate([d_gate, d_up], axis=1).astype(jnp.bfloat16)
    back_rows = lax.dot_general(
        dgate_up, w_gu, (((1,), (1,)), ((), ())), preferred_element_type=jnp.float32
    )
    return back_rows.astype(jnp.bfloat16)


def doc_backward(block, scale_val):
    query_blk, grad_blk, key_blk, value_blk = block
    doc_len = query_blk.shape[0]
    heads_here = query_blk.shape[1]
    causal = jnp.arange(doc_len)[:, None] >= jnp.arange(doc_len)[None, :]
    scores = (
        jnp.einsum("qhd,kd->hqk", query_blk, key_blk, preferred_element_type=jnp.float32)
        * scale_val
    )
    scores = jnp.where(causal[None], scores, -jnp.inf)
    top = jnp.max(scores, axis=-1, keepdims=True)
    expo = jnp.exp(scores - top)
    probs = expo / jnp.sum(expo, axis=-1, keepdims=True)
    probs_b = probs.astype(jnp.bfloat16)
    dprob = jnp.einsum("qhd,kd->hqk", grad_blk, value_blk, preferred_element_type=jnp.float32)
    delta = jnp.sum(probs * dprob, axis=-1, keepdims=True)
    dscore = (probs * (dprob - delta)).astype(jnp.bfloat16)
    dquery = (
        jnp.einsum("hqk,kd->qhd", dscore, key_blk, preferred_element_type=jnp.float32) * scale_val
    ).astype(jnp.bfloat16)
    dkey = (
        jnp.einsum("hqk,qhd->kd", dscore, query_blk, preferred_element_type=jnp.float32) * scale_val
    ).astype(jnp.bfloat16)
    dvalue = jnp.einsum(
        "hqk,qhd->kd", probs_b, grad_blk, preferred_element_type=jnp.float32
    ).astype(jnp.bfloat16)
    return jnp.concatenate(
        [dquery.reshape(doc_len, heads_here * key_blk.shape[1]), dkey, dvalue], axis=1
    )


def body(
    queries,
    keys,
    values,
    out_grad,
    q_weight,
    k_weight,
    v_weight,
    resid_grad,
    moe_input,
    expert_ids,
    route_weights,
    w_gate_up,
    w_down,
):
    row_count = lax.axis_size("row")
    heads_here = queries.shape[1] // HEAD_DIM
    group_size = HEADS // KV_HEADS
    kv_index = lax.axis_index("row") * heads_here // group_size
    key_head = lax.dynamic_slice_in_dim(keys, kv_index * HEAD_DIM, HEAD_DIM, 1)
    value_head = lax.dynamic_slice_in_dim(values, kv_index * HEAD_DIM, HEAD_DIM, 1)
    wk_local = lax.dynamic_slice_in_dim(k_weight, kv_index * HEAD_DIM, HEAD_DIM, 1)
    wv_local = lax.dynamic_slice_in_dim(v_weight, kv_index * HEAD_DIM, HEAD_DIM, 1)
    wcat_local = jnp.concatenate([q_weight, wk_local, wv_local], axis=1)
    wcat_whole = lax.all_gather(wcat_local, "col", axis=0, tiled=True)
    tok_rows = queries.shape[0]
    doc_count = tok_rows // DOC
    query_docs = queries.reshape(doc_count, DOC, heads_here, HEAD_DIM)
    grad_docs = out_grad.reshape(doc_count, DOC, heads_here, HEAD_DIM)
    key_docs = key_head.reshape(doc_count, DOC, HEAD_DIM)
    value_docs = value_head.reshape(doc_count, DOC, HEAD_DIM)
    dqkv = lax.map(
        partial(doc_backward, scale_val=HEAD_DIM ** (-0.5)),
        (query_docs, grad_docs, key_docs, value_docs),
    )
    dqkv = dqkv.reshape(tok_rows, dqkv.shape[-1])
    moe_rows = tok_rows // row_count
    term = lax.dot_general(
        dqkv, wcat_whole, (((1,), (1,)), ((), ())), preferred_element_type=jnp.float32
    )
    head_grad = lax.psum_scatter(
        lax.optimization_barrier(term.astype(jnp.bfloat16))
        .astype(jnp.float32)
        .astype(jnp.bfloat16),
        "row",
        scatter_dimension=0,
        tiled=True,
    ).astype(jnp.float32)
    layer_grad = head_grad + resid_grad.astype(jnp.float32)
    row_grad = layer_grad.astype(jnp.bfloat16)
    width = row_grad.shape[1]
    section_count = lax.axis_size("section")
    col_count = lax.axis_size("col")
    n_experts = section_count * row_count * col_count
    capacity = max(2, 9 * moe_rows * TOPK // (8 * n_experts))
    flat_ids = expert_ids.reshape(-1)
    onehot = (flat_ids[:, None] == jnp.arange(n_experts, dtype=jnp.int32)[None, :]).astype(
        jnp.int32
    )
    ranks = jnp.sum(jnp.cumsum(onehot, axis=0) * onehot, axis=1) - 1
    slots = flat_ids * capacity + ranks
    source = jnp.arange(moe_rows * TOPK, dtype=jnp.int32) // TOPK
    send_grads = (
        jnp.zeros((n_experts * capacity, width), jnp.bfloat16).at[slots].set(row_grad[source])
    )
    send_rows = (
        jnp.zeros((n_experts * capacity, width), jnp.bfloat16).at[slots].set(moe_input[source])
    )
    w_gu = w_gate_up[0]
    w_dn = w_down[0]

    def run_expert(grads_in, rows_in):
        lead = grads_in.shape[:-1]
        result = expert_math(rows_in.reshape(-1, width), grads_in.reshape(-1, width), w_gu, w_dn)
        return result.reshape(lead + (width,))

    def direct_work(pieces):
        result = run_expert(pieces[0], pieces[1])
        return cut_exchange(result, ("section", "row", "col"), 2, 0, 0)

    returned = items_in_groups(
        (
            send_grads.reshape(n_experts, capacity, width),
            send_rows.reshape(n_experts, capacity, width),
        ),
        ("section", "row", "col"),
        0,
        0,
        direct_work,
        1,
        1,
    )
    returned = returned.reshape(n_experts * capacity, width)
    pair_rows = returned[slots].astype(jnp.float32).reshape(moe_rows, TOPK, width)
    combined = jnp.sum(pair_rows * route_weights[:, :, None], axis=1)
    return combined.astype(jnp.bfloat16)


def solution(mesh):
    return jax.shard_map(
        body,
        mesh=mesh,
        in_specs=(
            P(("section", "col"), "row"),
            P(("section", "col"), None),
            P(("section", "col"), None),
            P(("section", "col"), "row"),
            P("col", "row"),
            P("col", None),
            P("col", None),
            P(("section", "row", "col"), None),
            P(("section", "row", "col"), None),
            P(("section", "row", "col"), None),
            P(("section", "row", "col"), None),
            P(("section", "row", "col"), None, None),
            P(("section", "row", "col"), None, None),
        ),
        out_specs=P(("section", "row", "col"), None),
        check_vma=False,
    )
```

profile of v0, /device:TPU:19, one launch (start us, length us, event | category | flops | bytes accessed | tf_op | source)
XLA Modules:
  0.0 611.9 jit_solution(16594846713916485419)
XLA Ops:
  16.2 61.2 %while.10 = (s32[]{:T(128)}, bf16[2,1024,512]{2,1,0:T(8,128)(2,1)}, bf16[2,1024,128]{2,1,0:T(8,128)(2,1)}, bf16[2,1024,2,128]{3,2,1,0:T(2,128)(2,1)}, bf16[2,102...) while((s32[]{:T(128)}, bf16[2,1024,512]{2,1,0:T(8,128)(2,1)}, ...), condition=%wide.region_7.8_spmd, body=%wide.region_3.7_spmd.sunk | while | flops 2716728320 | bytes 108840672 | solution.py:143
  16.2 2.9 constant_dynamic-slice_fusion.7
  20.4 8.0 %fusion.93 = (f32[2,1024]{1,0:T(2,128)S(1)}, f32[2,1024,1024]{1,2,0:T(8,128)}) fusion(pred[1024,1024]{0,1:T(8,128)(4,1)} %iota_compare_fusion.5, bf16[1,1024,2,128]{3,2,1,0:T(2,128)(2,1)} %get-tuple-element.118, bf16[2,1024,128]{2,1,0:T(8,128)(2,1)} %get-tuple-element.139, s32[]{:T(128)} %get-tuple-element.130), kind=kOutput, calls=%fused_computation.104.clone.1 | convolution fusion | flops 545260544 | bytes 10232320 | tf_op jit(solution)/shard_map/while/body/eval_jaxpr/sub | solution.py:92
  28.3 5.1 fusion.95
  46.8 2.9 constant_dynamic-slice_fusion.7
  51.0 7.9 %fusion.93 = (f32[2,1024]{1,0:T(2,128)S(1)}, f32[2,1024,1024]{1,2,0:T(8,128)}) fusion(pred[1024,1024]{0,1:T(8,128)(4,1)} %iota_compare_fusion.5, bf16[1,1024,2,128]{3,2,1,0:T(2,128)(2,1)} %get-tuple-element.118, bf16[2,1024,128]{2,1,0:T(8,128)(2,1)} %get-tuple-element.139, s32[]{:T(128)} %get-tuple-element.130), kind=kOutput, calls=%fused_computation.104.clone.1 | convolution fusion | flops 545260544 | bytes 10232320 | tf_op jit(solution)/shard_map/while/body/eval_jaxpr/sub | solution.py:92
  58.8 5.0 fusion.95
  77.4 10.0 %convolution_convert_fusion = bf16[2048,2048]{1,0:T(8,128)(2,1)} fusion(bf16[2048,512]{1,0:T(8,128)(2,1)} %bitcast.155, bf16[2048,512]{1,0:T(8,128)(2,1)} %all-gather.2.cloned.1.call-done), kind=kOutput, calls=%fused_computation.54 | convolution fusion | flops 4299161600 | bytes 12582912 | tf_op jit(solution)/shard_map/dot_general | solution.py:149
  93.2 23.6 %scatter_custom_fusion.1 = bf16[1152,2048]{1,0:T(8,128)(2,1)} fusion(s32[1024]{0:T(1024)S(1)} %bitcast.150, bf16[128,2048]{1,0:T(8,128)(2,1)} %param.23, s32[1024]{0:T(1024)S(1)} %broadcast_clamp_fusion.1, bf16[]{:T(256)} %constant.65.clone.1), kind=kCustom, calls=%fused_computation.60 | custom fusion | bytes 4719104 | tf_op jit(solution)/shard_map/scatter | solution.py:178
  116.8 8.2 %reshape.152 = bf16[128,9,2048]{2,1,0:T(8,128)(2,1)} reshape(bf16[1152,2048]{1,0:T(8,128)(2,1)} %scatter_custom_fusion.1) | data formatting | bytes 9437184 | tf_op jit(solution)/shard_map/reshape | solution.py:195
  125.0 19.3 %all-to-all-start.1 = ((bf16[128,9,2048]{2,1,0:T(8,128)(2,1)}), bf16[128,9,2048]{2,1,0:T(8,128)(2,1)}, u32[]{:S(2)}, u32[]{:S(2)}) async-start(bf16[128,9,2048]{2,1,0:T(8,128)(2,1)} %reshape.152), calls=%async_computation.2 | async-start | bytes 16777216 | tf_op jit(solution)/shard_map/all_to_all | solution.py:55
  144.3 121.4 %reduce-scatter.2.cloned.1.call-done = bf16[128,2048]{1,0:T(8,128)(2,1)} async-done(((bf16[2048,2048]{1,0:T(8,128)(2,1)}), bf16[128,2048]{1,0:T(8,128)(2,1)}) %reduce-scatter.2.cloned.1.call-update) | async-done | bytes 524304 | tf_op jit(solution)/shard_map/reduce_scatter | solution.py:152
  267.9 23.2 %scatter_custom_fusion = bf16[1152,2048]{1,0:T(8,128)(2,1)} fusion(s32[1024]{0:T(1024)S(1)} %bitcast.151, bf16[128,2048]{1,0:T(8,128)(2,1)} %add_convert_fusion, s32[1024]{0:T(1024)S(1)} %broadcast_clamp_fusion.1, bf16[]{:T(256)} %constant.65.clone.1), kind=kCustom, calls=%fused_computation.62 | custom fusion | bytes 4719104 | tf_op jit(solution)/shard_map/scatter | solution.py:175
  291.0 8.1 %reshape.150 = bf16[128,9,2048]{2,1,0:T(8,128)(2,1)} reshape(bf16[1152,2048]{1,0:T(8,128)(2,1)} %scatter_custom_fusion) | data formatting | bytes 9437184 | tf_op jit(solution)/shard_map/reshape | solution.py:194
  299.1 12.3 %all-to-all-start = ((bf16[128,9,2048]{2,1,0:T(8,128)(2,1)}), bf16[128,9,2048]{2,1,0:T(8,128)(2,1)}, u32[]{:S(2)}, u32[]{:S(2)}) async-start(bf16[128,9,2048]{2,1,0:T(8,128)(2,1)} %reshape.150), calls=%async_computation.1 | async-start | bytes 16777216 | tf_op jit(solution)/shard_map/all_to_all | solution.py:55
  311.4 8.4 %reshape.153 = bf16[1152,2048]{1,0:T(8,128)(2,1)} reshape(bf16[128,9,2048]{2,1,0:T(8,128)(2,1)} %all-to-all-done.1) | data formatting | bytes 9437184 | tf_op jit(solution)/shard_map/reshape | solution.py:185
  319.8 13.7 %fusion.45 = f32[1152,1536]{0,1:T(8,128)} fusion(bf16[1152,2048]{1,0:T(8,128)(2,1)} %reshape.153, bf16[1,2048,1536]{2,1,0:T(8,128)(2,1)} %param.26), kind=kOutput, calls=%fused_computation.57 | convolution fusion | flops 7247757312 | bytes 18087936 | tf_op jit(solution)/shard_map/dot_general | solution.py:65
  333.6 90.6 %all-to-all-done = bf16[128,9,2048]{2,1,0:T(8,128)(2,1)} async-done(((bf16[128,9,2048]{2,1,0:T(8,128)(2,1)}), bf16[128,9,2048]{2,1,0:T(8,128)(2,1)}, u32[]{:S(2)}, u32[]{:S(2)}) %all-to-all-start) | async-done | bytes 4718624 | tf_op jit(solution)/shard_map/all_to_all | solution.py:55
  424.1 8.5 %reshape.151 = bf16[1152,2048]{1,0:T(8,128)(2,1)} reshape(bf16[128,9,2048]{2,1,0:T(8,128)(2,1)} %all-to-all-done) | data formatting | bytes 9437184 | tf_op jit(solution)/shard_map/reshape | solution.py:185
  432.6 8.5 %fusion.53 = (bf16[1152,768]{0,1:T(8,128)(2,1)S(1)}, bf16[1152,768]{0,1:T(8,128)(2,1)S(1)}) fusion(f32[1152,1536]{0,1:T(8,128)} %fusion.45, bf16[1152,2048]{1,0:T(8,128)(2,1)} %reshape.151, bf16[1,768,2048]{2,1,0:T(8,128)(2,1)S(1)} %copy-done), kind=kOutput, calls=%fused_computation.67 | convolution fusion | flops 3635380224 | bytes 18481152 | tf_op jit(solution)/shard_map/dot_general | solution.py:68
  441.1 12.1 %convolution_convert_fusion.1 = bf16[1152,2048]{1,0:T(8,128)(2,1)} fusion(bf16[1,2048,1536]{2,1,0:T(8,128)(2,1)} %param.26, bf16[1152,768]{0,1:T(8,128)(2,1)S(1)} %get-tuple-element.69, bf16[1152,768]{0,1:T(8,128)(2,1)S(1)} %get-tuple-element.68), kind=kOutput, calls=%fused_computation.55 | convolution fusion | flops 7257194496 | bytes 14548992 | tf_op jit(solution)/shard_map/dot_general | solution.py:75
  453.3 8.1 %reshape_reshape.6 = bf16[128,1,9,2048]{3,2,0,1:T(8,128)(2,1)} reshape(bf16[1152,2048]{1,0:T(8,128)(2,1)} %convolution_convert_fusion.1) | data formatting | bytes 9437184 | tf_op jit(solution)/shard_map/reshape;reshape | solution.py:17
  461.4 4.7 slice_bitcast_fusion.1
  466.0 11.5 %all-to-all-start.2 = ((bf16[128,1,4,2048]{3,2,1,0:T(4,128)(2,1)}), bf16[128,1,4,2048]{3,2,1,0:T(4,128)(2,1)}, u32[]{:S(2)}, u32[]{:S(2)}) async-start(bf16[128,1,4,2048]{3,2,1,0:T(4,128)(2,1)} %slice_bitcast_fusion.1), calls=%async_computation.3 | async-start | bytes 4194304 | tf_op jit(solution)/shard_map/all_to_all | solution.py:38
  477.5 7.6 %slice_bitcast_fusion = bf16[128,1,5,2048]{3,2,1,0:T(8,128)(2,1)} fusion(bf16[128,1,9,2048]{3,2,0,1:T(8,128)(2,1)} %reshape_reshape.6), kind=kLoop, calls=%fused_computation.59 | loop fusion | bytes 5242880 | tf_op jit(solution)/shard_map/split | solution.py:36
  485.2 19.2 %all-to-all-done.2 = bf16[128,1,4,2048]{3,2,1,0:T(4,128)(2,1)} async-done(((bf16[128,1,4,2048]{3,2,1,0:T(4,128)(2,1)}), bf16[128,1,4,2048]{3,2,1,0:T(4,128)(2,1)}, u32[]{:S(2)}, u32[]{:S(2)}) %all-to-all-start.2) | async-done | bytes 2097184 | tf_op jit(solution)/shard_map/all_to_all | solution.py:38
  504.3 7.9 %all-to-all-start.3 = ((bf16[128,1,5,2048]{3,2,1,0:T(8,128)(2,1)}), bf16[128,1,5,2048]{3,2,1,0:T(8,128)(2,1)}, u32[]{:S(2)}, u32[]{:S(2)}) async-start(bf16[128,1,5,2048]{3,2,1,0:T(8,128)(2,1)} %slice_bitcast_fusion), calls=%async_computation.4 | async-start | bytes 8388608 | tf_op jit(solution)/shard_map/all_to_all | solution.py:38
  512.4 55.4 %all-to-all-done.3 = bf16[128,1,5,2048]{3,2,1,0:T(8,128)(2,1)} async-done(((bf16[128,1,5,2048]{3,2,1,0:T(8,128)(2,1)}), bf16[128,1,5,2048]{3,2,1,0:T(8,128)(2,1)}, u32[]{:S(2)}, u32[]{:S(2)}) %all-to-all-start.3) | async-done | bytes 2621472 | tf_op jit(solution)/shard_map/all_to_all | solution.py:38
  567.7 9.4 %pad_maximum_fusion = bf16[128,1,9,2048]{3,2,1,0:T(8,128)(2,1)} fusion(bf16[128,1,5,2048]{3,2,1,0:T(8,128)(2,1)} %all-to-all-done.3, bf16[128,1,4,2048]{3,2,1,0:T(4,128)(2,1)} %all-to-all-done.2), kind=kLoop, calls=%fused_computation.51 | loop fusion | flops 9437184 | bytes 9437184 | tf_op jit(solution)/shard_map/concatenate | solution.py:39
  577.1 8.4 %reshape_reshape.7 = bf16[1152,2048]{1,0:T(8,128)(2,1)} reshape(bf16[128,1,9,2048]{3,2,1,0:T(8,128)(2,1)} %pad_maximum_fusion) | data formatting | bytes 9437184 | tf_op jit(solution)/shard_map/reshape;reshape | solution.py:204
  585.5 11.8 %gather_fusion = bf16[1024,2048]{1,0:T(8,128)(2,1)} fusion(bf16[1152,2048]{1,0:T(8,128)(2,1)} %reshape_reshape.7, s32[1024]{0:T(1024)S(1)} %broadcast_clamp_fusion), kind=kCustom, calls=%fused_computation.2 | custom fusion | bytes 8392704 | tf_op jit(solution)/shard_map/gather | solution.py:205
  597.3 7.3 %fusion.43 = bf16[128,2048]{1,0:T(8,128)(2,1)} fusion(bf16[1024,2048]{1,0:T(8,128)(2,1)} %gather_fusion, f32[128,8]{1,0:T(8,128)S(1)} %copy.58), kind=kLoop, calls=%fused_computation.53 | loop fusion | flops 6029312 | bytes 4722688 | tf_op jit(solution)/shard_map/reduce_sum | solution.py:206
  (79 shorter events, 46.6 us)
Async XLA Ops:
  6.5 426.1 %copy-start = (bf16[1,768,2048]{2,1,0:T(8,128)(2,1)S(1)}, bf16[1,768,2048]{2,1,0:T(8,128)(2,1)}, u32[]{:S(2)}) copy-start(bf16[1,768,2048]{2,1,0:T(8,128)(2,1)} %param.27) | copy-start | bytes 9437188
  6.5 70.9 %all-gather.2.cloned.1.call-start = ((), (), s32[]{:S(2)}) async-start(), calls=%async_computation.5 | async-start | bytes 2621440 | tf_op jit(solution)/shard_map/all_gather | solution.py:136
  9.5 256.3 %reduce-scatter.2.cloned.1.call-start = ((), (), s32[]{:S(2)}) async-start(), calls=%async_computation.6 | async-start | bytes 8912896 | tf_op jit(solution)/shard_map/reduce_scatter | solution.py:152
  28.3 5.1 slice-start
  28.3 6.2 %slice-start.1 = ((s8[8388608]{0:T(1024)(128)(4,1)}), s8[4194304]{0:T(1024)(128)(4,1)S(1)}, s32[]{:S(2)}) async-start(s8[8388608]{0:T(1024)(128)(4,1)} %bitcast.145), calls=%async_computation.8 | async-start | bytes 8388608 | tf_op jit(solution)/shard_map/while
  34.6 2.5 copy-start.3
  37.0 1.0 copy-start.1
  37.0 2.6 copy-start.2
  58.8 5.1 slice-start
  58.8 6.1 slice-start.1
  64.9 2.5 copy-start.3
  67.4 1.0 copy-start.1
  67.4 2.6 copy-start.2
  87.4 0.7 copy-start.5
  88.7 0.8 copy-start.4
  125.0 174.1 %all-to-all-start.1 = ((bf16[128,9,2048]{2,1,0:T(8,128)(2,1)}), bf16[128,9,2048]{2,1,0:T(8,128)(2,1)}, u32[]{:S(2)}, u32[]{:S(2)}) async-start(bf16[128,9,2048]{2,1,0:T(8,128)(2,1)} %reshape.152), calls=%async_computation.2 | async-start | bytes 16777216 | tf_op jit(solution)/shard_map/all_to_all | solution.py:55
  299.1 125.0 %all-to-all-start = ((bf16[128,9,2048]{2,1,0:T(8,128)(2,1)}), bf16[128,9,2048]{2,1,0:T(8,128)(2,1)}, u32[]{:S(2)}, u32[]{:S(2)}) async-start(bf16[128,9,2048]{2,1,0:T(8,128)(2,1)} %reshape.150), calls=%async_computation.1 | async-start | bytes 16777216 | tf_op jit(solution)/shard_map/all_to_all | solution.py:55
  466.0 38.3 %all-to-all-start.2 = ((bf16[128,1,4,2048]{3,2,1,0:T(4,128)(2,1)}), bf16[128,1,4,2048]{3,2,1,0:T(4,128)(2,1)}, u32[]{:S(2)}, u32[]{:S(2)}) async-start(bf16[128,1,4,2048]{3,2,1,0:T(4,128)(2,1)} %slice_bitcast_fusion.1), calls=%async_computation.3 | async-start | bytes 4194304 | tf_op jit(solution)/shard_map/all_to_all | solution.py:38
  485.2 27.1 %copy-start.6 = (f32[128,8]{0,1:T(8,128)S(1)}, f32[128,8]{0,1:T(8,128)}, u32[]{:S(2)}) copy-start(f32[128,8]{0,1:T(8,128)} %param.25) | copy-start | bytes 12292
  504.3 63.4 %all-to-all-start.3 = ((bf16[128,1,5,2048]{3,2,1,0:T(8,128)(2,1)}), bf16[128,1,5,2048]{3,2,1,0:T(8,128)(2,1)}, u32[]{:S(2)}, u32[]{:S(2)}) async-start(bf16[128,1,5,2048]{3,2,1,0:T(8,128)(2,1)} %slice_bitcast_fusion), calls=%async_computation.4 | async-start | bytes 8388608 | tf_op jit(solution)/shard_map/all_to_all | solution.py:38
Sparse Core Ops, SparseCore 0:
  9.6 32.0 all-gather.1
  87.6 178.1 reduce-scatter.1
where the time goes:
time: 622 us; the launch traced here: 612 us
  waiting for transfers between devices  287 us (46%)
  local copies, waits for them, and re-layouts  149 us (24%)
  matrix products  78 us (13%)
  starting transfers between devices  51.1 us (8%)
  other arithmetic  33 us (5%)
  between operations  14 us (2%)
    reduce_scatter x1, waiting for transfers between devices, body(): lax.psum_scatter(lax.optimization_barrier(term.astype(jnp.bfloat16)).asty...  121 us
    all_to_all x2, waiting for transfers between devices, items_in_groups(): lax.all_to_all(group, axis, split_axis=split_dim, concat_axis=concat_dim,...  90.6 us
    all_to_all x2, waiting for transfers between devices, cut_exchange(): lax.all_to_all(piece, axis, split_axis=0, concat_axis=0, tiled=True)  74.5 us
    scatter x2, local copies, waits for them, and re-layouts, body(): jnp.zeros((n_experts * capacity, width), jnp.bfloat16).at[slots]  46.7 us
    all_to_all x2, starting transfers between devices, items_in_groups(): lax.all_to_all(group, axis, split_axis=split_dim, concat_axis=concat_dim,...  31.6 us
    all_to_all x2, starting transfers between devices, cut_exchange(): lax.all_to_all(piece, axis, split_axis=0, concat_axis=0, tiled=True)  19.4 us
    sub x2, matrix products, doc_backward(): expo = jnp.exp(scores - top)  15.8 us
    dot_general x1, matrix products, expert_math(): gate_up = jnp.dot(rows_in, w_gu, preferred_element_type=jnp.float32)  13.7 us
  transfers between devices with their start and end apart: 6, of which 4 were waited for; matrix products, arithmetic and copies ran while one was open for 27% of the time, Pallas kernels for 0%

commit v1 on v0

v1 whole, which is shorter than its diff:
```python
import math

import jax
import jax.numpy as jnp
from jax import lax
from jax.experimental import pallas as pl
from jax.experimental.pallas import tpu as pltpu
from jax.sharding import PartitionSpec as P

HEADS = 32
KV_HEADS = 4
HD = 128
TOPK = 8
DOC = 1024
D = 2048
FF = 768
CAP = 9
TOK = 128
NE = 128
N_Y = 4
N_Z = 4
HALF = 1024
MSG = 72
CHUNK = 32
ROWS = CHUNK * CAP
BF = jnp.bfloat16
F32 = jnp.float32
VMEM_LIMIT = 60 * 1024 * 1024
ALL = ("section", "row", "col")
SCALE = HD ** (-0.5)


def params(steps):
    return pltpu.CompilerParams(
        dimension_semantics=("arbitrary",) * steps, vmem_limit_bytes=VMEM_LIMIT
    )


def dot_nn(a, b):
    return lax.dot_general(a, b, (((1,), (0,)), ((), ())), preferred_element_type=F32)


def dot_nt(a, b):
    return lax.dot_general(a, b, (((1,), (1,)), ((), ())), preferred_element_type=F32)


def pack_half(x, pick, out_ref, scr):
    main = pick[: NE * 8]
    last = pick[NE * 8 :]
    for jj in range(0, 8, 2):
        got = dot_nn(main, x[:, jj * 128 : (jj + 2) * 128])
        for q in range(2):
            piece = got[:, q * 128 : (q + 1) * 128].reshape(NE, 8, 128)
            out_ref[:, (jj + q) * 8 : (jj + q + 1) * 8, :] = piece.astype(BF)
    ninth = dot_nn(last, x)
    for jj in range(8):
        scr[pl.ds(jj, NE, stride=8), :] = ninth[:, jj * 128 : (jj + 1) * 128]
    out_ref[:, 64:72, :] = scr[...].reshape(NE, 8, 128).astype(BF)


def slot_tables(ids_ref):
    e_iota = lax.broadcasted_iota(jnp.int32, (NE, TOK), 0)
    named = jnp.zeros((NE, TOK), F32)
    for k in range(TOPK):
        named = named + jnp.where(ids_ref[k : k + 1, :] == e_iota, 1.0, 0.0)
    before = jnp.where(
        lax.broadcasted_iota(jnp.int32, (TOK, TOK), 0)
        < lax.broadcasted_iota(jnp.int32, (TOK, TOK), 1),
        1.0,
        0.0,
    ).astype(BF)
    count = dot_nn(named.astype(BF), before)
    return e_iota, jnp.where(named > 0.5, count, -1.0)


def spread_matrix():
    r = lax.broadcasted_iota(jnp.int32, (NE * 8, NE), 0)
    c = lax.broadcasted_iota(jnp.int32, (NE * 8, NE), 1)
    return jnp.where(lax.shift_right_logical(r, 3) == c, 1.0, 0.0).astype(BF)


def slot_number():
    r = lax.broadcasted_iota(jnp.int32, (NE * 8, TOK), 0)
    return jnp.bitwise_and(r, 7).astype(F32)


def route_pack_kernel(ids_ref, x_ref, pick_ref, out_ref, scr):
    @pl.when(pl.program_id(0) == 0)
    def _():
        _, count = slot_tables(ids_ref)
        wide = dot_nn(spread_matrix(), count.astype(BF))
        pick_ref[: NE * 8] = jnp.where(wide == slot_number(), 1.0, 0.0).astype(BF)
        pick_ref[NE * 8 :] = jnp.where(count == 8.0, 1.0, 0.0).astype(BF)

    pack_half(x_ref[...], pick_ref[...], out_ref, scr)


def route_pack(ids_t, x):
    return pl.pallas_call(
        route_pack_kernel,
        grid=(2,),
        in_specs=[
            pl.BlockSpec((TOPK, TOK), lambda n: (0, 0)),
            pl.BlockSpec((TOK, HALF), lambda n: (0, n)),
        ],
        out_specs=[
            pl.BlockSpec((NE * CAP, TOK), lambda n: (0, 0)),
            pl.BlockSpec((NE, MSG, 128), lambda n: (0, n, 0)),
        ],
        out_shape=[
            jax.ShapeDtypeStruct((NE * CAP, TOK), BF),
            jax.ShapeDtypeStruct((NE, 2 * MSG, 128), BF),
        ],
        scratch_shapes=[pltpu.VMEM((NE * 8, 128), F32)],
        compiler_params=params(1),
        name="route_pack",
    )(ids_t, x)


def weights_kernel(ids_ref, rw_ref, out_ref):
    e_iota, count = slot_tables(ids_ref)
    weight = jnp.zeros((NE, TOK), F32)
    for k in range(TOPK):
        weight = weight + jnp.where(ids_ref[k : k + 1, :] == e_iota, rw_ref[k : k + 1, :], 0.0)
    high = weight.astype(BF)
    low = (weight - high.astype(F32)).astype(BF)
    spread = spread_matrix()
    hit = dot_nn(spread, count.astype(BF)) == slot_number()
    for i, part in enumerate((high, low)):
        wide = jnp.where(hit, dot_nn(spread, part), 0.0)
        out_ref[i * TOK : (i + 1) * TOK, : NE * 8] = wide.T.astype(BF)
        tail = jnp.where(count == 8.0, part.astype(F32), 0.0)
        out_ref[i * TOK : (i + 1) * TOK, NE * 8 :] = tail.T.astype(BF)


def combine_weights(ids_t, rw_t):
    return pl.pallas_call(
        weights_kernel,
        out_shape=jax.ShapeDtypeStruct((2 * TOK, NE * CAP), BF),
        compiler_params=pltpu.CompilerParams(vmem_limit_bytes=VMEM_LIMIT),
        name="combine_weights",
    )(ids_t, rw_t)


def attention_kernel(kv_ref, q_ref, g_ref, k_ref, v_ref, out_ref, dk_acc, dv_acc):
    del kv_ref
    blk = 256
    factor = SCALE * math.log2(math.e)
    k_all = k_ref[...]
    k_t = k_all.astype(F32).T.astype(BF)
    allowed = lax.broadcasted_iota(jnp.int32, (blk, blk), 0) <= lax.broadcasted_iota(
        jnp.int32, (blk, blk), 1
    )
    first = True
    for h in range(2):
        for qb in reversed(range(DOC // blk)):
            length = (qb + 1) * blk
            q = q_ref[qb * blk : length, h * HD : (h + 1) * HD]
            g = g_ref[qb * blk : length, h * HD : (h + 1) * HD]
            k = k_ref[:length, :]
            v = v_ref[:length, :]
            s = dot_nt(k, q)
            diag = jnp.where(allowed, s[length - blk :], -jnp.inf)
            s = jnp.concatenate([s[: length - blk], diag], axis=0) if qb else diag
            top = jnp.max(s, axis=0, keepdims=True)
            expo = jnp.exp2((s - top) * factor)
            inv = 1.0 / jnp.sum(expo, axis=0, keepdims=True)
            dprob = dot_nt(v, g)
            delta = jnp.sum(expo * dprob, axis=0, keepdims=True) * inv
            probs = expo * inv
            dscore = (probs * (dprob - delta)).astype(BF)
            probs_b = probs.astype(BF)
            dq_t = dot_nn(k_t[:, :length], dscore) * SCALE
            dq = dq_t.T.astype(BF)
            y = (2 * qb) % N_Y
            z = qb // 2
            out_ref[y, z, :, h * HD : (h + 1) * HD] = dq[:128]
            out_ref[y + 1, z, :, h * HD : (h + 1) * HD] = dq[128:]
            dk = dot_nn(dscore, q)
            dv = dot_nn(probs_b, g)
            if first:
                dk_acc[...] = dk
                dv_acc[...] = dv
                first = False
            else:
                dk_acc[:length] += dk
                dv_acc[:length] += dv
    for b in range(DOC // 128):
        out_ref[b % N_Y, b // N_Y, :, 2 * HD : 3 * HD] = (
            dk_acc[b * 128 : (b + 1) * 128, :] * SCALE
        ).astype(BF)
        out_ref[b % N_Y, b // N_Y, :, 3 * HD :] = dv_acc[b * 128 : (b + 1) * 128, :].astype(BF)


def attention(kv_index, queries, out_grad, keys, values):
    docs = queries.shape[0] // DOC
    wide = pl.BlockSpec((DOC, 2 * HD), lambda d, kv: (d, 0))
    thin = pl.BlockSpec((DOC, HD), lambda d, kv: (d, kv[0]))
    return pl.pallas_call(
        attention_kernel,
        grid_spec=pltpu.PrefetchScalarGridSpec(
            num_scalar_prefetch=1,
            grid=(docs,),
            in_specs=[wide, wide, thin, thin],
            out_specs=pl.BlockSpec((N_Y, N_Z // docs, TOK, 4 * HD), lambda d, kv: (0, d, 0, 0)),
            scratch_shapes=[pltpu.VMEM((DOC, HD), F32), pltpu.VMEM((DOC, HD), F32)],
        ),
        out_shape=jax.ShapeDtypeStruct((N_Y, N_Z, TOK, 4 * HD), BF),
        compiler_params=params(1),
        name="attention",
    )(kv_index, queries, out_grad, keys, values)


def project_kernel(x_ref, wq_ref, wkv_ref, out_ref, kv_scr):
    @pl.when(pl.program_id(0) == 0)
    def _():
        total = x_ref[0, :, 2 * HD :].astype(F32)
        for y in range(1, N_Y):
            total = total + x_ref[y, :, 2 * HD :].astype(F32)
        kv_scr[...] = total.astype(BF)

    acc = dot_nt(kv_scr[...], wkv_ref[0])
    for y in range(N_Y):
        acc = acc + dot_nt(x_ref[y, :, : 2 * HD], wq_ref[y, 0])
    out_ref[...] = acc.astype(BF)


def project(x, wq, wkv):
    tokens = x.shape[1]
    cols, width = wq.shape[1], wq.shape[2]
    return pl.pallas_call(
        project_kernel,
        grid=(cols,),
        in_specs=[
            pl.BlockSpec((N_Y, tokens, 4 * HD), lambda n: (0, 0, 0)),
            pl.BlockSpec((N_Y, 1, width, 2 * HD), lambda n: (0, n, 0, 0)),
            pl.BlockSpec((1, width, 2 * HD), lambda n: (n, 0, 0)),
        ],
        out_specs=pl.BlockSpec((tokens, width), lambda n: (0, n)),
        out_shape=jax.ShapeDtypeStruct((tokens, cols * width), BF),
        scratch_shapes=[pltpu.VMEM((tokens, 2 * HD), BF)],
        compiler_params=params(1),
        name="project",
    )(x, wq, wkv)


def sum_pack_kernel(parts_ref, resid_ref, pick_ref, out_ref, scr):
    total = resid_ref[...].astype(F32)
    for z in range(N_Z):
        total = total + parts_ref[z].astype(F32)
    pack_half(total.astype(BF), pick_ref[...], out_ref, scr)


def sum_pack(parts, resid, pick):
    return pl.pallas_call(
        sum_pack_kernel,
        grid=(2,),
        in_specs=[
            pl.BlockSpec((N_Z, TOK, HALF), lambda n: (0, 0, n)),
            pl.BlockSpec((TOK, HALF), lambda n: (0, n)),
            pl.BlockSpec((NE * CAP, TOK), lambda n: (0, 0)),
        ],
        out_specs=pl.BlockSpec((NE, MSG, 128), lambda n: (0, n, 0)),
        out_shape=jax.ShapeDtypeStruct((NE, 2 * MSG, 128), BF),
        scratch_shapes=[pltpu.VMEM((NE * 8, 128), F32)],
        compiler_params=params(1),
        name="sum_pack",
    )(parts, resid, pick)


def unpack_rows(msg_ref, rows, scr):
    main = CHUNK * 8
    for n in range(2):
        scr[...] = msg_ref[:, n * MSG + 64 : (n + 1) * MSG, :].astype(F32).reshape(main, 128)
        for jj in range(8):
            at = (n * 8 + jj) * 128
            piece = msg_ref[:, n * MSG + jj * 8 : n * MSG + (jj + 1) * 8, :]
            rows[:main, at : at + 128] = piece.reshape(main, 128)
            rows[main:, at : at + 128] = scr[pl.ds(jj, CHUNK, stride=8), :].astype(BF)


def gate_up_kernel(msg_ref, w_ref, out_ref, rows, scr):
    unpack_rows(msg_ref, rows, scr)
    gate_up = dot_nn(rows[...], w_ref[...])
    gate = gate_up[:, :FF]
    up = gate_up[:, FF:]
    sigm = 1.0 / (1.0 + jnp.exp(-gate))
    out_ref[:, :FF] = up * sigm * (1.0 + gate * (1.0 - sigm))
    out_ref[:, FF:] = gate * sigm


def gate_factors(msg, w_gu):
    steps = NE // CHUNK
    return pl.pallas_call(
        gate_up_kernel,
        grid=(steps,),
        in_specs=[
            pl.BlockSpec((CHUNK, 2 * MSG, 128), lambda i: (i, 0, 0)),
            pl.BlockSpec((D, 2 * FF), lambda i: (0, 0)),
        ],
        out_specs=pl.BlockSpec((ROWS, 2 * FF), lambda i: (i, 0)),
        out_shape=jax.ShapeDtypeStruct((NE * CAP, 2 * FF), F32),
        scratch_shapes=[pltpu.VMEM((ROWS, D), BF), pltpu.VMEM((CHUNK * 8, 128), F32)],
        compiler_params=params(1),
        name="gate_factors",
    )(msg, w_gu)


def expert_kernel(msg_ref, fac_ref, wd_ref, w_ref, out_ref, rows, scr):
    main = CHUNK * 8
    unpack_rows(msg_ref, rows, scr)
    dhidden = dot_nt(rows[...], wd_ref[...])
    d_gate = (dhidden * fac_ref[:, :FF]).astype(BF)
    d_up = (dhidden * fac_ref[:, FF:]).astype(BF)
    both = jnp.concatenate([d_gate, d_up], axis=1)
    for n in range(2):
        back = dot_nt(both, w_ref[n * HALF : (n + 1) * HALF, :])
        for jj in range(8):
            piece = back[:main, jj * 128 : (jj + 1) * 128].reshape(CHUNK, 8, 128)
            out_ref[:, n * MSG + jj * 8 : n * MSG + (jj + 1) * 8, :] = piece.astype(BF)
            scr[pl.ds(jj, CHUNK, stride=8), :] = back[main:, jj * 128 : (jj + 1) * 128]
        out_ref[:, n * MSG + 64 : (n + 1) * MSG, :] = scr[...].reshape(CHUNK, 8, 128).astype(BF)


def expert_back(msg, factors, w_dn, w_gu):
    steps = NE // CHUNK
    return pl.pallas_call(
        expert_kernel,
        grid=(steps,),
        in_specs=[
            pl.BlockSpec((CHUNK, 2 * MSG, 128), lambda i: (i, 0, 0)),
            pl.BlockSpec((ROWS, 2 * FF), lambda i: (i, 0)),
            pl.BlockSpec((FF, D), lambda i: (0, 0)),
            pl.BlockSpec((D, 2 * FF), lambda i: (0, 0)),
        ],
        out_specs=pl.BlockSpec((CHUNK, 2 * MSG, 128), lambda i: (i, 0, 0)),
        out_shape=jax.ShapeDtypeStruct((NE, 2 * MSG, 128), BF),
        scratch_shapes=[pltpu.VMEM((ROWS, D), BF), pltpu.VMEM((CHUNK * 8, 128), F32)],
        compiler_params=params(1),
        name="expert_back",
    )(msg, factors, w_dn, w_gu)


def combine_kernel(msg_ref, w_ref, out_ref, scr):
    scr[...] = msg_ref[:, 64:72, :].astype(F32).reshape(NE * 8, 128)
    w_main = w_ref[:, : NE * 8]
    w_last = w_ref[:, NE * 8 :]
    for jj in range(8):
        piece = msg_ref[:, jj * 8 : (jj + 1) * 8, :].reshape(NE * 8, 128)
        ninth = scr[pl.ds(jj, NE, stride=8), :].astype(BF)
        both = dot_nn(w_main, piece) + dot_nn(w_last, ninth)
        out_ref[:, jj * 128 : (jj + 1) * 128] = (both[:TOK] + both[TOK:]).astype(BF)


def combine(msg, weights):
    return pl.pallas_call(
        combine_kernel,
        grid=(2,),
        in_specs=[
            pl.BlockSpec((NE, MSG, 128), lambda n: (0, n, 0)),
            pl.BlockSpec((2 * TOK, NE * CAP), lambda n: (0, 0)),
        ],
        out_specs=pl.BlockSpec((TOK, HALF), lambda n: (0, n)),
        out_shape=jax.ShapeDtypeStruct((TOK, D), BF),
        scratch_shapes=[pltpu.VMEM((NE * 8, 128), F32)],
        compiler_params=params(1),
        name="combine",
    )(msg, weights)


def exchange(x, axis, groups=None):
    return lax.all_to_all(
        x, axis, split_axis=0, concat_axis=0, tiled=True, axis_index_groups=groups
    )


def body(
    queries,
    keys,
    values,
    out_grad,
    q_weight,
    k_weight,
    v_weight,
    resid_grad,
    moe_input,
    expert_ids,
    route_weights,
    w_gate_up,
    w_down,
):
    n_col = lax.axis_size("col")
    row_of = [[N_Y * z + y for y in range(N_Y)] for z in range(N_Z)]
    same_y = [[N_Y * z + y for z in range(N_Z)] for y in range(N_Y)]
    planes = [[n_col * r + c for r in rows for c in range(n_col)] for rows in row_of]
    kv_index = lax.axis_index("row") // N_Y

    wk = lax.dynamic_slice_in_dim(k_weight, kv_index * HD, HD, 1)
    wv = lax.dynamic_slice_in_dim(v_weight, kv_index * HD, HD, 1)
    wq_all = lax.all_gather(
        q_weight, ("row", "col"), axis=0, tiled=True, axis_index_groups=planes
    ).reshape(N_Y, n_col, D // n_col, 2 * HD)
    wkv_all = lax.all_gather(
        jnp.concatenate([wk, wv], axis=1), "col", axis=0, tiled=True
    ).reshape(n_col, D // n_col, 2 * HD)

    ids_t = expert_ids.T
    pick, send_rows = route_pack(ids_t, moe_input)
    got_rows = exchange(send_rows, ALL)
    weights = combine_weights(ids_t, route_weights.T)

    dqkv = attention(kv_index.reshape(1).astype(jnp.int32), queries, out_grad, keys, values)
    dqkv = exchange(dqkv.reshape(N_Y, N_Z * TOK, 4 * HD), "row", row_of)
    term = project(dqkv, wq_all, wkv_all)
    parts = exchange(term.reshape(N_Z, TOK, D), "row", same_y)

    got_grads = exchange(sum_pack(parts, resid_grad, pick), ALL)
    w_gu = w_gate_up.reshape(D, 2 * FF)
    factors = gate_factors(got_rows, w_gu)
    back = expert_back(got_grads, factors, w_down.reshape(FF, D), w_gu)
    return combine(exchange(back, ALL), weights)


def solution(mesh):
    return jax.shard_map(
        body,
        mesh=mesh,
        in_specs=(
            P(("section", "col"), "row"),
            P(("section", "col"), None),
            P(("section", "col"), None),
            P(("section", "col"), "row"),
            P("col", "row"),
            P("col", None),
            P("col", None),
            P(ALL, None),
            P(ALL, None),
            P(ALL, None),
            P(ALL, None),
            P(ALL, None, None),
            P(ALL, None, None),
        ),
        out_specs=P(ALL, None),
        check_vma=False,
    )
```

time: 622 us -> 374 us (0.60); the launches traced: 612 us -> 373 us
  local copies, waits for them, and re-layouts: 149 us -> 2.35 us
  matrix products: 78 us -> 0 us
  Pallas kernels: 0 us -> 72.7 us
  waiting for transfers between devices: 287 us -> 227 us
  other arithmetic: 33 us -> 0.73 us
  blocking collectives: 0 us -> 28.9 us
  starting transfers between devices: 51.1 us -> 27.5 us
    reduce_scatter x1 -> x0, waiting for transfers between devices: 121 us -> none  [body(): lax.psum_scatter(lax.optimization_barrier(term.astype(jnp.bfloat16)).asty...]
    pallas_call x0 -> x8, Pallas kernels: none -> 72.7 us  [the longest x1 20.9 us: expert_back(): pl.pallas_call(expert_kernel, grid=(steps,), in_specs=[pl.BlockSpec((CHUN...]
    dot_general x12 -> x0, matrix products: 62.2 us -> none  [the longest x1 13.7 us: expert_math(): gate_up = jnp.dot(rows_in, w_gu, preferred_element_type=jnp.float32)]
    scatter x2 -> x0, local copies, waits for them, and re-layouts: 46.7 us -> none  [body(): jnp.zeros((n_experts * capacity, width), jnp.bfloat16).at[slots]]
    reshape x6 -> x0, local copies, waits for them, and re-layouts: 37.5 us -> none  [the longest x1 8.47 us: run_expert(): grads_in.reshape(-1, width)]
    all_gather x1 -> x2, waiting for transfers between devices: 0.02 us -> 36.7 us  [the longest x1 36.7 us: body(): lax.all_gather(q_weight, ('row', 'col'), axis=0, tiled=True, axis_index_g...]
    all_to_all x0 -> x1, blocking collectives: none -> 28.9 us  [exchange(): lax.all_to_all(x, axis, split_axis=0, concat_axis=0, tiled=True, axis_ind...]
    all_to_all x4, waiting for transfers between devices: 165 us -> 190 us  [exchange(): lax.all_to_all(x, axis, split_axis=0, concat_axis=0, tiled=True, axis_ind...]
  transfers between devices with their start and end apart: 6 -> 6, of which waited for: 4 -> 5; matrix products, arithmetic and copies ran while one was open for 27% -> 0% of each run, Pallas kernels for 0% -> 11%
where the time goes in v1:
time: 374 us; the launch traced here: 373 us
  waiting for transfers between devices  227 us (61%)
  Pallas kernels  72.7 us (19%)
  blocking collectives  28.9 us (8%)
  starting transfers between devices  27.5 us (7%)
  between operations  13.4 us (4%)
    all_to_all x4, waiting for transfers between devices, exchange(): lax.all_to_all(x, axis, split_axis=0, concat_axis=0, tiled=True, axis_ind...  190 us
    all_gather x1, waiting for transfers between devices, body(): lax.all_gather(q_weight, ('row', 'col'), axis=0, tiled=True, axis_index_g...  36.7 us
    all_to_all x1, blocking collectives, exchange(): lax.all_to_all(x, axis, split_axis=0, concat_axis=0, tiled=True, axis_ind...  28.9 us
    all_to_all x4, starting transfers between devices, exchange(): lax.all_to_all(x, axis, split_axis=0, concat_axis=0, tiled=True, axis_ind...  27.5 us
    pallas_call x1, Pallas kernels, expert_back(): pl.pallas_call(expert_kernel, grid=(steps,), in_specs=[pl.BlockSpec((CHUN...  20.9 us
    pallas_call x1, Pallas kernels, attention(): pl.pallas_call(attention_kernel, grid_spec=pltpu.PrefetchScalarGridSpec(n...  15.1 us
    pallas_call x1, Pallas kernels, gate_factors(): pl.pallas_call(gate_up_kernel, grid=(steps,), in_specs=[pl.BlockSpec((CHU...  12.8 us
  transfers between devices with their start and end apart: 6, of which 5 were waited for; matrix products, arithmetic and copies ran while one was open for 0% of the time, Pallas kernels for 11%

profile of v1, /device:TPU:19, one launch (start us, length us, event | category | flops | bytes accessed | tf_op | source)
XLA Modules:
  0.0 372.9 jit_solution(13158183709145476300)
XLA Ops:
  6.5 0.0 all-gather.5.cloned.1.call-start
  6.5 1.0 constant_dynamic-slice_fusion
  7.5 0.7 pad_maximum_fusion
  8.3 0.0 all-gather.5.cloned.1.call-update
  8.3 0.0 all-gather.3.cloned.1.call-start
  8.3 0.7 all-gather.3.cloned.1.call-update
  9.0 15.1 %attention.1 = bf16[4,4,128,512]{3,2,1,0:T(8,128)(2,1)} custom-call(s32[1]{0:T(128)} %bitcast.kv_ref, bf16[2048,256]{1,0:T(8,128)(2,1)} %q_ref.1, bf16[2048,256]{1,0:T(8,128)(2,1)} %g_ref.1, bf16[2048,512]{1,0:T(8,128)(2,1)} %k_ref.1, bf16[2048,512]{1,0:T(8,128)(2,1)} %v_ref.1), custom_call_target="tpu_custom_call" | custom-call | tf_op jit(solution)/shard_map/attention/pallas_call | solution.py:199
  24.1 28.9 %all_to_all.25.x_ref = bf16[4,512,512]{2,1,0:T(8,128)(2,1)} all-to-all(bf16[4,512,512]{2,1,0:T(8,128)(2,1)} %bitcast.12), channel_id=1, replica_groups={{0,4,8,12},{16,20,24,28},{32,36,40,44},{48,52,56,60},{1,5,9,13},{17,21,..., dimensions={0} | all-to-all | bytes 4194304 | tf_op jit(solution)/shard_map/all_to_all | solution.py:372
  53.0 0.0 all-gather.5.cloned.1.call-done
  53.0 36.7 %all-gather.3.cloned.1.call-done = bf16[8192,256]{1,0:T(8,128)(2,1)} async-done(((bf16[512,256]{1,0:T(8,128)(2,1)}), bf16[8192,256]{1,0:T(8,128)(2,1)}) %all-gather.3.cloned.1.call-update) | async-done | bytes 4194320 | tf_op jit(solution)/shard_map/all_gather | solution.py:400
  89.7 7.2 %project.1 = bf16[512,2048]{1,0:T(8,128)(2,1)} custom-call(bf16[4,512,512]{2,1,0:T(8,128)(2,1)} %all_to_all.25.x_ref, bf16[4,4,512,256]{3,2,1,0:T(8,128)(2,1)} %bitcast.13, bf16[4,512,256]{2,1,0:T(8,128)(2,1)} %bitcast.15), custom_call_target="tpu_custom_call" | custom-call | tf_op jit(solution)/shard_map/project/pallas_call | solution.py:231
  97.0 4.1 %all-to-all-start.1 = ((bf16[4,128,2048]{2,1,0:T(8,128)(2,1)}), bf16[4,128,2048]{2,1,0:T(8,128)(2,1)S(1)}, u32[]{:S(2)}, u32[]{:S(2)}) async-start(bf16[4,128,2048]{2,1,0:T(8,128)(2,1)} %bitcast.11), calls=%async_computation.1 | async-start | bytes 4194304 | tf_op jit(solution)/shard_map/all_to_all | solution.py:372
  101.1 4.5 %route_pack.1 = (bf16[1152,128]{1,0:T(8,128)(2,1)}, bf16[128,144,128]{2,1,0:T(8,128)(2,1)}) custom-call(s32[8,128]{1,0:T(8,128)} %bitcast.16, bf16[128,2048]{1,0:T(8,128)(2,1)} %x_ref.1), custom_call_target="tpu_custom_call" | custom-call | tf_op jit(solution)/shard_map/route_pack/pallas_call | solution.py:99
  105.6 21.0 %all-to-all-done.1.parts_ref = bf16[4,128,2048]{2,1,0:T(8,128)(2,1)S(1)} async-done(((bf16[4,128,2048]{2,1,0:T(8,128)(2,1)}), bf16[4,128,2048]{2,1,0:T(8,128)(2,1)S(1)}, u32[]{:S(2)}, u32[]{:S(2)}) %all-to-all-start.1) | async-done | bytes 2097184 | tf_op jit(solution)/shard_map/all_to_all | solution.py:372
  126.5 0.0 copy-start
  126.5 1.4 copy-done
  127.9 9.0 %all-to-all-start.3 = ((bf16[128,144,128]{2,1,0:T(8,128)(2,1)}), bf16[128,144,128]{2,1,0:T(8,128)(2,1)}, u32[]{:S(2)}, u32[]{:S(2)}) async-start(bf16[128,144,128]{2,1,0:T(8,128)(2,1)} %get-tuple-element.8), calls=%async_computation.3 | async-start | bytes 9437184 | tf_op jit(solution)/shard_map/all_to_all | solution.py:372
  136.9 4.7 %sum_pack.1 = bf16[128,144,128]{2,1,0:T(8,128)(2,1)} custom-call(bf16[4,128,2048]{2,1,0:T(8,128)(2,1)} %copy-done, bf16[128,2048]{1,0:T(8,128)(2,1)} %resid_ref.1, bf16[1152,128]{1,0:T(8,128)(2,1)} %get-tuple-element.7.pick_ref), custom_call_target="tpu_custom_call" | custom-call | tf_op jit(solution)/shard_map/sum_pack/pallas_call | solution.py:255
  141.6 58.2 %all-to-all-done.3.msg_ref = bf16[128,144,128]{2,1,0:T(8,128)(2,1)} async-done(((bf16[128,144,128]{2,1,0:T(8,128)(2,1)}), bf16[128,144,128]{2,1,0:T(8,128)(2,1)}, u32[]{:S(2)}, u32[]{:S(2)}) %all-to-all-start.3) | async-done | bytes 4718624 | tf_op jit(solution)/shard_map/all_to_all | solution.py:372
  199.8 7.3 %all-to-all-start.2 = ((bf16[128,144,128]{2,1,0:T(8,128)(2,1)}), bf16[128,144,128]{2,1,0:T(8,128)(2,1)}, u32[]{:S(2)}, u32[]{:S(2)}) async-start(bf16[128,144,128]{2,1,0:T(8,128)(2,1)} %sum_pack.1), calls=%async_computation.2 | async-start | bytes 9437184 | tf_op jit(solution)/shard_map/all_to_all | solution.py:372
  207.1 12.8 %gate_factors.1.fac_ref = f32[1152,1536]{1,0:T(8,128)} custom-call(bf16[128,144,128]{2,1,0:T(8,128)(2,1)} %all-to-all-done.3.msg_ref, bf16[2048,1536]{1,0:T(8,128)(2,1)} %bitcast.9), custom_call_target="tpu_custom_call" | custom-call | tf_op jit(solution)/shard_map/gate_factors/pallas_call | solution.py:294
  219.9 50.1 %all-to-all-done.2.msg_ref = bf16[128,144,128]{2,1,0:T(8,128)(2,1)} async-done(((bf16[128,144,128]{2,1,0:T(8,128)(2,1)}), bf16[128,144,128]{2,1,0:T(8,128)(2,1)}, u32[]{:S(2)}, u32[]{:S(2)}) %all-to-all-start.2) | async-done | bytes 4718624 | tf_op jit(solution)/shard_map/all_to_all | solution.py:372
  270.0 20.9 %expert_back.1 = bf16[128,144,128]{2,1,0:T(8,128)(2,1)} custom-call(bf16[128,144,128]{2,1,0:T(8,128)(2,1)} %all-to-all-done.2.msg_ref, f32[1152,1536]{1,0:T(8,128)} %gate_factors.1.fac_ref, bf16[768,2048]{1,0:T(8,128)(2,1)} %bitcast.14, bf16[2048,1536]{1,0:T(8,128)(2,1)} %bitcast.10), custom_call_target="tpu_custom_call" | custom-call | tf_op jit(solution)/shard_map/expert_back/pallas_call | solution.py:327
  290.9 7.0 %all-to-all-start.4 = ((bf16[128,144,128]{2,1,0:T(8,128)(2,1)}), bf16[128,144,128]{2,1,0:T(8,128)(2,1)}, u32[]{:S(2)}, u32[]{:S(2)}) async-start(bf16[128,144,128]{2,1,0:T(8,128)(2,1)} %expert_back.1), calls=%async_computation.4 | async-start | bytes 9437184 | tf_op jit(solution)/shard_map/all_to_all | solution.py:372
  297.9 2.2 combine_weights.1.w_ref
  300.1 60.6 %all-to-all-done.4.msg_ref = bf16[128,144,128]{2,1,0:T(8,128)(2,1)} async-done(((bf16[128,144,128]{2,1,0:T(8,128)(2,1)}), bf16[128,144,128]{2,1,0:T(8,128)(2,1)}, u32[]{:S(2)}, u32[]{:S(2)}) %all-to-all-start.4) | async-done | bytes 4718624 | tf_op jit(solution)/shard_map/all_to_all | solution.py:372
  360.8 5.3 %combine.1 = bf16[128,2048]{1,0:T(8,128)(2,1)} custom-call(bf16[128,144,128]{2,1,0:T(8,128)(2,1)} %all-to-all-done.4.msg_ref, bf16[256,1152]{1,0:T(8,128)(2,1)} %combine_weights.1.w_ref), custom_call_target="tpu_custom_call" | custom-call | tf_op jit(solution)/shard_map/combine/pallas_call | solution.py:356
Async XLA Ops:
  6.5 46.5 %all-gather.5.cloned.1.call-start = ((), (), s32[]{:S(2)}) async-start(), calls=%async_computation.6 | async-start | bytes 1310720 | tf_op jit(solution)/shard_map/all_gather | solution.py:403
  8.3 81.4 %all-gather.3.cloned.1.call-start = ((), (), s32[]{:S(2)}) async-start(), calls=%async_computation.5 | async-start | bytes 4456448 | tf_op jit(solution)/shard_map/all_gather | solution.py:400
  97.0 29.6 %all-to-all-start.1 = ((bf16[4,128,2048]{2,1,0:T(8,128)(2,1)}), bf16[4,128,2048]{2,1,0:T(8,128)(2,1)S(1)}, u32[]{:S(2)}, u32[]{:S(2)}) async-start(bf16[4,128,2048]{2,1,0:T(8,128)(2,1)} %bitcast.11), calls=%async_computation.1 | async-start | bytes 4194304 | tf_op jit(solution)/shard_map/all_to_all | solution.py:372
  126.5 1.4 copy-start
  127.9 71.9 %all-to-all-start.3 = ((bf16[128,144,128]{2,1,0:T(8,128)(2,1)}), bf16[128,144,128]{2,1,0:T(8,128)(2,1)}, u32[]{:S(2)}, u32[]{:S(2)}) async-start(bf16[128,144,128]{2,1,0:T(8,128)(2,1)} %get-tuple-element.8), calls=%async_computation.3 | async-start | bytes 9437184 | tf_op jit(solution)/shard_map/all_to_all | solution.py:372
  199.8 70.2 %all-to-all-start.2 = ((bf16[128,144,128]{2,1,0:T(8,128)(2,1)}), bf16[128,144,128]{2,1,0:T(8,128)(2,1)}, u32[]{:S(2)}, u32[]{:S(2)}) async-start(bf16[128,144,128]{2,1,0:T(8,128)(2,1)} %sum_pack.1), calls=%async_computation.2 | async-start | bytes 9437184 | tf_op jit(solution)/shard_map/all_to_all | solution.py:372
  290.9 69.8 %all-to-all-start.4 = ((bf16[128,144,128]{2,1,0:T(8,128)(2,1)}), bf16[128,144,128]{2,1,0:T(8,128)(2,1)}, u32[]{:S(2)}, u32[]{:S(2)}) async-start(bf16[128,144,128]{2,1,0:T(8,128)(2,1)} %expert_back.1), calls=%async_computation.4 | async-start | bytes 9437184 | tf_op jit(solution)/shard_map/all_to_all | solution.py:372
Sparse Core Ops, SparseCore 0:
  9.0 24.0 all-gather.4
  35.2 54.4 all-gather.2

commit v2 on v1

--- a/solution.py
+++ b/solution.py
@@ -36,6 +36,10 @@
     )
 
 
+def cost(us):
+    return pl.CostEstimate(flops=int(us * 1.1e9), transcendentals=0, bytes_accessed=int(us * 3e6))
+
+
 def dot_nn(a, b):
     return lax.dot_general(a, b, (((1,), (0,)), ((), ())), preferred_element_type=F32)
 
@@ -84,36 +88,24 @@
     return jnp.bitwise_and(r, 7).astype(F32)
 
 
-def route_pack_kernel(ids_ref, x_ref, pick_ref, out_ref, scr):
-    @pl.when(pl.program_id(0) == 0)
-    def _():
-        _, count = slot_tables(ids_ref)
-        wide = dot_nn(spread_matrix(), count.astype(BF))
-        pick_ref[: NE * 8] = jnp.where(wide == slot_number(), 1.0, 0.0).astype(BF)
-        pick_ref[NE * 8 :] = jnp.where(count == 8.0, 1.0, 0.0).astype(BF)
-
-    pack_half(x_ref[...], pick_ref[...], out_ref, scr)
+def route_pack_kernel(ids_ref, x_ref, pick_ref, out0, out1, scr):
+    _, count = slot_tables(ids_ref)
+    wide = dot_nn(spread_matrix(), count.astype(BF))
+    pick_ref[: NE * 8] = jnp.where(wide == slot_number(), 1.0, 0.0).astype(BF)
+    pick_ref[NE * 8 :] = jnp.where(count == 8.0, 1.0, 0.0).astype(BF)
+    for n, out in enumerate((out0, out1)):
+        pack_half(x_ref[:, n * HALF : (n + 1) * HALF], pick_ref[...], out, scr)
 
 
 def route_pack(ids_t, x):
+    half = jax.ShapeDtypeStruct((NE, MSG, 128), BF)
     return pl.pallas_call(
         route_pack_kernel,
-        grid=(2,),
-        in_specs=[
-            pl.BlockSpec((TOPK, TOK), lambda n: (0, 0)),
-            pl.BlockSpec((TOK, HALF), lambda n: (0, n)),
-        ],
-        out_specs=[
-            pl.BlockSpec((NE * CAP, TOK), lambda n: (0, 0)),
-            pl.BlockSpec((NE, MSG, 128), lambda n: (0, n, 0)),
-        ],
-        out_shape=[
-            jax.ShapeDtypeStruct((NE * CAP, TOK), BF),
-            jax.ShapeDtypeStruct((NE, 2 * MSG, 128), BF),
-        ],
+        out_shape=[jax.ShapeDtypeStruct((NE * CAP, TOK), BF), half, half],
         scratch_shapes=[pltpu.VMEM((NE * 8, 128), F32)],
-        compiler_params=params(1),
+        compiler_params=pltpu.CompilerParams(vmem_limit_bytes=VMEM_LIMIT),
         name="route_pack",
+        cost_estimate=cost(5),
     )(ids_t, x)
 
 
@@ -139,11 +131,13 @@
         out_shape=jax.ShapeDtypeStruct((2 * TOK, NE * CAP), BF),
         compiler_params=pltpu.CompilerParams(vmem_limit_bytes=VMEM_LIMIT),
         name="combine_weights",
+        cost_estimate=cost(2.2),
     )(ids_t, rw_t)
 
 
-def attention_kernel(kv_ref, q_ref, g_ref, k_ref, v_ref, out_ref, dk_acc, dv_acc):
-    del kv_ref
+def attention_kernel(
+    at_ref, q_ref, g_ref, k_ref, v_ref, out0, out1, out2, out3, dk_acc, dv_acc, out_ref
+):
     blk = 256
     factor = SCALE * math.log2(math.e)
     k_all = k_ref[...]
@@ -190,128 +184,150 @@
             dk_acc[b * 128 : (b + 1) * 128, :] * SCALE
         ).astype(BF)
         out_ref[b % N_Y, b // N_Y, :, 3 * HD :] = dv_acc[b * 128 : (b + 1) * 128, :].astype(BF)
-
-
-def attention(kv_index, queries, out_grad, keys, values):
+    for k, out in enumerate((out0, out1, out2, out3)):
+        out[...] = out_ref[jnp.bitwise_and(at_ref[1] + k, N_Y - 1)]
+
+
+def attention(place, queries, out_grad, keys, values):
     docs = queries.shape[0] // DOC
-    wide = pl.BlockSpec((DOC, 2 * HD), lambda d, kv: (d, 0))
-    thin = pl.BlockSpec((DOC, HD), lambda d, kv: (d, kv[0]))
+    wide = pl.BlockSpec((DOC, 2 * HD), lambda d, at: (d, 0))
+    thin = pl.BlockSpec((DOC, HD), lambda d, at: (d, at[0]))
+    piece = pl.BlockSpec((N_Z // docs, TOK, 4 * HD), lambda d, at: (d, 0, 0))
     return pl.pallas_call(
         attention_kernel,
         grid_spec=pltpu.PrefetchScalarGridSpec(
             num_scalar_prefetch=1,
             grid=(docs,),
             in_specs=[wide, wide, thin, thin],
-            out_specs=pl.BlockSpec((N_Y, N_Z // docs, TOK, 4 * HD), lambda d, kv: (0, d, 0, 0)),
-            scratch_shapes=[pltpu.VMEM((DOC, HD), F32), pltpu.VMEM((DOC, HD), F32)],
+            out_specs=[piece] * N_Y,
+            scratch_shapes=[
+                pltpu.VMEM((DOC, HD), F32),
+                pltpu.VMEM((DOC, HD), F32),
+                pltpu.VMEM((N_Y, N_Z // docs, TOK, 4 * HD), BF),
+            ],
         ),
-        out_shape=jax.ShapeDtypeStruct((N_Y, N_Z, TOK, 4 * HD), BF),
+        out_shape=[jax.ShapeDtypeStruct((N_Z, TOK, 4 * HD), BF)] * N_Y,
         compiler_params=params(1),
         name="attention",
-    )(kv_index, queries, out_grad, keys, values)
-
-
-def project_kernel(x_ref, wq_ref, wkv_ref, out_ref, kv_scr):
-    @pl.when(pl.program_id(0) == 0)
-    def _():
-        total = x_ref[0, :, 2 * HD :].astype(F32)
-        for y in range(1, N_Y):
-            total = total + x_ref[y, :, 2 * HD :].astype(F32)
-        kv_scr[...] = total.astype(BF)
-
-    acc = dot_nt(kv_scr[...], wkv_ref[0])
-    for y in range(N_Y):
-        acc = acc + dot_nt(x_ref[y, :, : 2 * HD], wq_ref[y, 0])
-    out_ref[...] = acc.astype(BF)
-
-
-def project(x, wq, wkv):
-    tokens = x.shape[1]
-    cols, width = wq.shape[1], wq.shape[2]
+        cost_estimate=cost(16),
+    )(place, queries, out_grad, keys, values)
+
+
+def project_kernel(at_ref, x0, x1, x2, x3, w0, w1, w2, w3, out0, out1, out2, out3, scr):
+    pieces = (x0, x1, x2, x3)
+    total = x0[:, 2 * HD :].astype(F32)
+    for x in pieces[1:]:
+        total = total + x[:, 2 * HD :].astype(F32)
+    total = total.astype(BF)
+    width = scr.shape[3]
+    for k, w_ref in enumerate((w0, w1, w2, w3)):
+        acc = dot_nt(total, w_ref[N_Y * width :])
+        for y, x in enumerate(pieces):
+            acc = acc + dot_nt(x[:, : 2 * HD], w_ref[y * width : (y + 1) * width])
+        col = jnp.bitwise_and(at_ref[3] - k, 3)
+        for z in range(N_Z):
+            scr[z, col] = acc[z * TOK : (z + 1) * TOK].astype(BF)
+    for k, out in enumerate((out0, out1, out2, out3)):
+        out[...] = scr[jnp.bitwise_and(at_ref[0] + k, N_Z - 1)]
+
+
+def project(place, pieces, weights):
+    width = weights[0].shape[0] // (N_Y + 1)
+    out = jax.ShapeDtypeStruct((len(weights), TOK, width), BF)
+    whole = pl.BlockSpec(memory_space=pltpu.VMEM)
     return pl.pallas_call(
         project_kernel,
-        grid=(cols,),
-        in_specs=[
-            pl.BlockSpec((N_Y, tokens, 4 * HD), lambda n: (0, 0, 0)),
-            pl.BlockSpec((N_Y, 1, width, 2 * HD), lambda n: (0, n, 0, 0)),
-            pl.BlockSpec((1, width, 2 * HD), lambda n: (n, 0, 0)),
-        ],
-        out_specs=pl.BlockSpec((tokens, width), lambda n: (0, n)),
-        out_shape=jax.ShapeDtypeStruct((tokens, cols * width), BF),
-        scratch_shapes=[pltpu.VMEM((tokens, 2 * HD), BF)],
-        compiler_params=params(1),
+        in_specs=[pl.BlockSpec(memory_space=pltpu.SMEM)] + [whole] * 8,
+        out_specs=[whole] * N_Z,
+        out_shape=[out] * N_Z,
+        scratch_shapes=[pltpu.VMEM((N_Z, len(weights), TOK, width), BF)],
+        compiler_params=pltpu.CompilerParams(vmem_limit_bytes=VMEM_LIMIT),
         name="project",
-    )(x, wq, wkv)
-
-
-def sum_pack_kernel(parts_ref, resid_ref, pick_ref, out_ref, scr):
-    total = resid_ref[...].astype(F32)
-    for z in range(N_Z):
-        total = total + parts_ref[z].astype(F32)
+        cost_estimate=cost(6),
+    )(place, *pieces, *weights)
+
+
+def sum_pack_kernel(at_ref, m0, m1, m2, m3, o0, o1, o2, o3, resid_ref, pick_ref, out_ref, scr):
+    blocks = []
+    for c in range(2):
+        mine, other = (
+            sum((x[c].astype(F32) for x in xs[1:]), xs[0][c].astype(F32))
+            for xs in ((m0, m1, m2, m3), (o0, o1, o2, o3))
+        )
+        for h in range(2):
+            blocks.append(jnp.where(at_ref[2] == h, mine, other))
+    total = resid_ref[...].astype(F32) + jnp.concatenate(blocks, axis=1)
     pack_half(total.astype(BF), pick_ref[...], out_ref, scr)
 
 
-def sum_pack(parts, resid, pick):
+def sum_pack(place, mine, other, resid, pick):
+    part = pl.BlockSpec((2, TOK, 256), lambda n, at: (n, 0, 0))
     return pl.pallas_call(
         sum_pack_kernel,
-        grid=(2,),
-        in_specs=[
-            pl.BlockSpec((N_Z, TOK, HALF), lambda n: (0, 0, n)),
-            pl.BlockSpec((TOK, HALF), lambda n: (0, n)),
-            pl.BlockSpec((NE * CAP, TOK), lambda n: (0, 0)),
-        ],
-        out_specs=pl.BlockSpec((NE, MSG, 128), lambda n: (0, n, 0)),
+        grid_spec=pltpu.PrefetchScalarGridSpec(
+            num_scalar_prefetch=1,
+            grid=(2,),
+            in_specs=[part] * 8
+            + [
+                pl.BlockSpec((TOK, HALF), lambda n, at: (0, n)),
+                pl.BlockSpec((NE * CAP, TOK), lambda n, at: (0, 0)),
+            ],
+            out_specs=pl.BlockSpec((NE, MSG, 128), lambda n, at: (0, n, 0)),
+            scratch_shapes=[pltpu.VMEM((NE * 8, 128), F32)],
+        ),
         out_shape=jax.ShapeDtypeStruct((NE, 2 * MSG, 128), BF),
-        scratch_shapes=[pltpu.VMEM((NE * 8, 128), F32)],
         compiler_params=params(1),
         name="sum_pack",
-    )(parts, resid, pick)
-
-
-def unpack_rows(msg_ref, rows, scr):
+        cost_estimate=cost(5.5),
+    )(place, *mine, *other, resid, pick)
+
+
+def unpack_rows(halves, rows, scr):
     main = CHUNK * 8
-    for n in range(2):
-        scr[...] = msg_ref[:, n * MSG + 64 : (n + 1) * MSG, :].astype(F32).reshape(main, 128)
+    for n, msg_ref in enumerate(halves):
+        scr[...] = msg_ref[:, 64:, :].astype(F32).reshape(main, 128)
         for jj in range(8):
             at = (n * 8 + jj) * 128
-            piece = msg_ref[:, n * MSG + jj * 8 : n * MSG + (jj + 1) * 8, :]
+            piece = msg_ref[:, jj * 8 : (jj + 1) * 8, :]
             rows[:main, at : at + 128] = piece.reshape(main, 128)
             rows[main:, at : at + 128] = scr[pl.ds(jj, CHUNK, stride=8), :].astype(BF)
 
 
-def gate_up_kernel(msg_ref, w_ref, out_ref, rows, scr):
-    unpack_rows(msg_ref, rows, scr)
+def gate_up_kernel(msg0, msg1, w_ref, out_ref, rows, scr):
+    unpack_rows((msg0, msg1), rows, scr)
     gate_up = dot_nn(rows[...], w_ref[...])
     gate = gate_up[:, :FF]
     up = gate_up[:, FF:]
     sigm = 1.0 / (1.0 + jnp.exp(-gate))
-    out_ref[:, :FF] = up * sigm * (1.0 + gate * (1.0 - sigm))
-    out_ref[:, FF:] = gate * sigm
-
-
-def gate_factors(msg, w_gu):
+    out_ref[:, :FF] = (up * sigm * (1.0 + gate * (1.0 - sigm))).astype(BF)
+    out_ref[:, FF:] = (gate * sigm).astype(BF)
+
+
+def gate_factors(halves, w_gu):
     steps = NE // CHUNK
     return pl.pallas_call(
         gate_up_kernel,
         grid=(steps,),
         in_specs=[
-            pl.BlockSpec((CHUNK, 2 * MSG, 128), lambda i: (i, 0, 0)),
+            pl.BlockSpec((CHUNK, MSG, 128), lambda i: (i, 0, 0)),
+            pl.BlockSpec((CHUNK, MSG, 128), lambda i: (i, 0, 0)),
             pl.BlockSpec((D, 2 * FF), lambda i: (0, 0)),
         ],
         out_specs=pl.BlockSpec((ROWS, 2 * FF), lambda i: (i, 0)),
-        out_shape=jax.ShapeDtypeStruct((NE * CAP, 2 * FF), F32),
+        out_shape=jax.ShapeDtypeStruct((NE * CAP, 2 * FF), BF),
         scratch_shapes=[pltpu.VMEM((ROWS, D), BF), pltpu.VMEM((CHUNK * 8, 128), F32)],
         compiler_params=params(1),
         name="gate_factors",
-    )(msg, w_gu)
-
-
-def expert_kernel(msg_ref, fac_ref, wd_ref, w_ref, out_ref, rows, scr):
+        cost_estimate=cost(12.5),
+    )(*halves, w_gu)
+
+
+def expert_kernel(msg0, msg1, fac_ref, wd_ref, w_ref, out_ref, rows, scr):
     main = CHUNK * 8
-    unpack_rows(msg_ref, rows, scr)
+    unpack_rows((msg0, msg1), rows, scr)
     dhidden = dot_nt(rows[...], wd_ref[...])
-    d_gate = (dhidden * fac_ref[:, :FF]).astype(BF)
-    d_up = (dhidden * fac_ref[:, FF:]).astype(BF)
+    d_gate = (dhidden * fac_ref[:, :FF].astype(F32)).astype(BF)
+    d_up = (dhidden * fac_ref[:, FF:].astype(F32)).astype(BF)
     both = jnp.concatenate([d_gate, d_up], axis=1)
     for n in range(2):
         back = dot_nt(both, w_ref[n * HALF : (n + 1) * HALF, :])
@@ -328,7 +344,8 @@
         expert_kernel,
         grid=(steps,),
         in_specs=[
-            pl.BlockSpec((CHUNK, 2 * MSG, 128), lambda i: (i, 0, 0)),
+            pl.BlockSpec((CHUNK, MSG, 128), lambda i: (i, 0, 0)),
+            pl.BlockSpec((CHUNK, MSG, 128), lambda i: (i, 1, 0)),
             pl.BlockSpec((ROWS, 2 * FF), lambda i: (i, 0)),
             pl.BlockSpec((FF, D), lambda i: (0, 0)),
             pl.BlockSpec((D, 2 * FF), lambda i: (0, 0)),
@@ -338,7 +355,8 @@
         scratch_shapes=[pltpu.VMEM((ROWS, D), BF), pltpu.VMEM((CHUNK * 8, 128), F32)],
         compiler_params=params(1),
         name="expert_back",
-    )(msg, factors, w_dn, w_gu)
+        cost_estimate=cost(20),
+    )(msg, msg, factors, w_dn, w_gu)
 
 
 def combine_kernel(msg_ref, w_ref, out_ref, scr):
@@ -365,6 +383,7 @@
         scratch_shapes=[pltpu.VMEM((NE * 8, 128), F32)],
         compiler_params=params(1),
         name="combine",
+        cost_estimate=cost(5.3),
     )(msg, weights)
 
 
@@ -390,31 +409,50 @@
     w_down,
 ):
     n_col = lax.axis_size("col")
-    row_of = [[N_Y * z + y for y in range(N_Y)] for z in range(N_Z)]
-    same_y = [[N_Y * z + y for z in range(N_Z)] for y in range(N_Y)]
-    planes = [[n_col * r + c for r in rows for c in range(n_col)] for rows in row_of]
-    kv_index = lax.axis_index("row") // N_Y
-
-    wk = lax.dynamic_slice_in_dim(k_weight, kv_index * HD, HD, 1)
-    wv = lax.dynamic_slice_in_dim(v_weight, kv_index * HD, HD, 1)
-    wq_all = lax.all_gather(
-        q_weight, ("row", "col"), axis=0, tiled=True, axis_index_groups=planes
-    ).reshape(N_Y, n_col, D // n_col, 2 * HD)
-    wkv_all = lax.all_gather(
-        jnp.concatenate([wk, wv], axis=1), "col", axis=0, tiled=True
-    ).reshape(n_col, D // n_col, 2 * HD)
+    row = lax.axis_index("row")
+    kv_index = row // N_Y
+    section = lax.axis_index("section")
+    place = jnp.stack([kv_index, row % N_Y, section, lax.axis_index("col")]).astype(jnp.int32)
+    others = range(1, N_Y)
+
+    def ahead_y(x, k):
+        hops = [(N_Y * z + y, N_Y * z + (y + k) % N_Y) for z in range(N_Z) for y in range(N_Y)]
+        return lax.ppermute(x, "row", hops)
+
+    def ahead_z(x, k):
+        hops = [(N_Y * z + y, N_Y * ((z + k) % N_Z) + y) for z in range(N_Z) for y in range(N_Y)]
+        return lax.ppermute(x, "row", hops)
+
+    def ahead_c(x, k):
+        return lax.ppermute(x, "col", [(c, (c + k) % n_col) for c in range(n_col)])
+
+    half = D // n_col // 2
+    wq = lax.dynamic_slice_in_dim(q_weight, section * half, half, 0)
+    wk = lax.dynamic_slice(k_weight, (section * half, kv_index * HD), (half, HD))
+    wv = lax.dynamic_slice(v_weight, (section * half, kv_index * HD), (half, HD))
+    w_own = jnp.concatenate(
+        [wq, *(ahead_y(wq, k) for k in others), jnp.concatenate([wk, wv], axis=1)], axis=0
+    )
+    w_mine = [w_own] + [ahead_c(w_own, k) for k in others]
+    w_other = [lax.ppermute(w, "section", [(0, 1), (1, 0)]) for w in w_mine]
 
     ids_t = expert_ids.T
-    pick, send_rows = route_pack(ids_t, moe_input)
-    got_rows = exchange(send_rows, ALL)
+    pick, *send_rows = route_pack(ids_t, moe_input)
+    got_rows = [exchange(half_rows, ALL) for half_rows in send_rows]
     weights = combine_weights(ids_t, route_weights.T)
 
-    dqkv = attention(kv_index.reshape(1).astype(jnp.int32), queries, out_grad, keys, values)
-    dqkv = exchange(dqkv.reshape(N_Y, N_Z * TOK, 4 * HD), "row", row_of)
-    term = project(dqkv, wq_all, wkv_all)
-    parts = exchange(term.reshape(N_Z, TOK, D), "row", same_y)
-
-    got_grads = exchange(sum_pack(parts, resid_grad, pick), ALL)
+    queries, _ = lax.optimization_barrier((queries, pick))
+    pieces = attention(place, queries, out_grad, keys, values)
+    pieces = [p.reshape(N_Z * TOK, 4 * HD) for p in pieces]
+    pieces = [pieces[0]] + [ahead_y(pieces[k], k) for k in others]
+
+    def head_half(weights):
+        parts = project(place, pieces, weights)
+        return [parts[0]] + [ahead_z(parts[k], k) for k in others]
+
+    head_mine = head_half(w_mine)
+    head_other = head_half(w_other)
+    got_grads = exchange(sum_pack(place, head_mine, head_other, resid_grad, pick), ALL)
     w_gu = w_gate_up.reshape(D, 2 * FF)
     factors = gate_factors(got_rows, w_gu)
     back = expert_back(got_grads, factors, w_down.reshape(FF, D), w_gu)

time: 374 us -> 302 us (0.81)
  waiting for transfers between devices: 227 us -> 157 us
  starting transfers between devices: 27.5 us -> 63.1 us
  blocking collectives: 28.9 us -> 0 us
  between operations: 13.4 us -> 0.19 us
  Pallas kernels: 72.7 us -> 76.8 us
    all_to_all x4, waiting for transfers between devices: 190 us -> 111 us  [exchange(): lax.all_to_all(x, axis, split_axis=0, concat_axis=0, tiled=True, axis_ind...]
    ppermute x0 -> x19, waiting for transfers between devices: none -> 46 us  [the longest x6 32.3 us: ahead_z(): return lax.ppermute(x, 'row', hops)]
    all_gather x2 -> x0, waiting for transfers between devices: 36.7 us -> none  [the longest x1 36.7 us: body(): lax.all_gather(q_weight, ('row', 'col'), axis=0, tiled=True, axis_index_g...]
    all_to_all x1 -> x0, blocking collectives: 28.9 us -> none  [exchange(): lax.all_to_all(x, axis, split_axis=0, concat_axis=0, tiled=True, axis_ind...]
    all_to_all x4, starting transfers between devices: 27.5 us -> 46.2 us  [exchange(): lax.all_to_all(x, axis, split_axis=0, concat_axis=0, tiled=True, axis_ind...]
    ppermute x0 -> x19, starting transfers between devices: none -> 16.9 us  [the longest x6 7.98 us: ahead_z(): return lax.ppermute(x, 'row', hops)]
    pallas_call x3 -> x4, Pallas kernels: 16.4 us -> 20 us  [the longest x2 9.95 us: project(): pl.pallas_call(project_kernel, in_specs=[pl.BlockSpec(memory_space=pltpu....]
  transfers between devices with their start and end apart: 6 -> 23, of which waited for: 5 -> 8; matrix products, arithmetic and copies ran while one was open for 0% -> 1% of each run, Pallas kernels for 11% -> 17%
where the time goes in v2:
time: 302 us; the launch traced here: 301 us
  waiting for transfers between devices  157 us (52%)
  Pallas kernels  76.8 us (25%)
  starting transfers between devices  63.1 us (21%)
  local copies, waits for them, and re-layouts  3.44 us (1%)
    all_to_all x4, waiting for transfers between devices, exchange(): lax.all_to_all(x, axis, split_axis=0, concat_axis=0, tiled=True, axis_ind...  111 us
    all_to_all x4, starting transfers between devices, exchange(): lax.all_to_all(x, axis, split_axis=0, concat_axis=0, tiled=True, axis_ind...  46.2 us
    ppermute x6, waiting for transfers between devices, ahead_z(): return lax.ppermute(x, 'row', hops)  32.3 us
    pallas_call x1, Pallas kernels, expert_back(): pl.pallas_call(expert_kernel, grid=(steps,), in_specs=[pl.BlockSpec((CHUN...  20.7 us
    pallas_call x1, Pallas kernels, attention(): pl.pallas_call(attention_kernel, grid_spec=pltpu.PrefetchScalarGridSpec(n...  15.9 us
    ppermute x6, waiting for transfers between devices, ahead_y(): return lax.ppermute(x, 'row', hops)  13.6 us
    pallas_call x1, Pallas kernels, gate_factors(): pl.pallas_call(gate_up_kernel, grid=(steps,), in_specs=[pl.BlockSpec((CHU...  12.7 us
    pallas_call x2, Pallas kernels, project(): pl.pallas_call(project_kernel, in_specs=[pl.BlockSpec(memory_space=pltpu....  9.95 us
  transfers between devices with their start and end apart: 23, of which 8 were waited for; matrix products, arithmetic and copies ran while one was open for 1% of the time, Pallas kernels for 17%

profile of v2, /device:TPU:19, one launch (start us, length us, event | category | flops | bytes accessed | tf_op | source)
XLA Modules:
  0.0 300.9 jit_solution(12284329577634014497)
XLA Ops:
  0.0 0.9 constant_dynamic-update-slice_fusion.3
  0.9 1.1 collective-permute-start.3
  2.3 0.9 collective-permute-start.5
  3.3 4.4 %route_pack.1 = (bf16[1152,128]{1,0:T(8,128)(2,1)}, bf16[128,72,128]{2,1,0:T(8,128)(2,1)}, bf16[128,72,128]{2,1,0:T(8,128)(2,1)}) custom-call(s32[8,128]{1,0:T(8,128)} %bitcast.18, bf16[128,2048]{1,0:T(8,128)(2,1)} %x_ref.1), custom_call_target="tpu_custom_call" | custom-call | flops 5500000256 | bytes 15000000 | tf_op jit(solution)/shard_map/route_pack/pallas_call | solution.py:102
  7.6 11.7 %all-to-all-start.1 = ((bf16[128,72,128]{2,1,0:T(8,128)(2,1)}), bf16[128,72,128]{2,1,0:T(8,128)(2,1)S(1)}, u32[]{:S(2)}, u32[]{:S(2)}) async-start(bf16[128,72,128]{2,1,0:T(8,128)(2,1)} %get-tuple-element.35), calls=%async_computation.1 | async-start | bytes 4718592 | tf_op jit(solution)/shard_map/all_to_all | solution.py:391
  19.9 15.9 %attention.1 = (bf16[4,128,512]{2,1,0:T(8,128)(2,1)}, bf16[4,128,512]{2,1,0:T(8,128)(2,1)}, bf16[4,128,512]{2,1,0:T(8,128)(2,1)}, bf16[4,128,512]{2,1,0:T(8,128)(2,1)}) custom-call(s32[4]{0:T(128)} %pad_add_fusion.at_ref, bf16[2048,256]{1,0:T(8,128)(2,1)} %q_ref, bf16[2048,256]{1,0:T(8,128)(2,1)} %g_ref.1, bf16[2048,512]{1,0:T(8,128)(2,1)} %k_ref.1, ...), custom_call_target="tpu_custom_call" | custom-call | flops 17600000000 | bytes 48000000 | tf_op jit(solution)/shard_map/attention/pallas_call | solution.py:196
  35.8 1.0 collective-permute-start
  37.6 0.8 dynamic_slice.11
  38.5 1.3 collective-permute-start.6
  39.8 0.9 collective-permute-start.7
  40.6 1.8 collective-permute-start.8
  43.0 13.6 %collective-permute-done.x1 = bf16[512,512]{1,0:T(8,128)(2,1)} collective-permute-done((bf16[512,512]{1,0:T(8,128)(2,1)}, bf16[512,512]{1,0:T(8,128)(2,1)}, u32[]{:S(2)}, u32[]{:S(2)}) %collective-permute-start) | collective-permute-done | bytes 524320 | tf_op jit(solution)/shard_map/ppermute | solution.py:420
  56.7 18.9 %all-to-all-start.2 = ((bf16[128,72,128]{2,1,0:T(8,128)(2,1)}), bf16[128,72,128]{2,1,0:T(8,128)(2,1)}, u32[]{:S(2)}, u32[]{:S(2)}) async-start(bf16[128,72,128]{2,1,0:T(8,128)(2,1)} %get-tuple-element.36), calls=%async_computation.2 | async-start | bytes 4718592 | tf_op jit(solution)/shard_map/all_to_all | solution.py:391
  76.7 5.0 %project.2 = (bf16[4,128,256]{2,1,0:T(8,128)(2,1)}, bf16[4,128,256]{2,1,0:T(8,128)(2,1)}, bf16[4,128,256]{2,1,0:T(8,128)(2,1)}, bf16[4,128,256]{2,1,0:T(8,128)(2,1)}) custom-call(s32[4]{0:T(128)} %pad_add_fusion.at_ref, bf16[512,512]{1,0:T(8,128)(2,1)} %bitcast.21, bf16[512,512]{1,0:T(8,128)(2,1)} %collective-permute-done.x1, bf16[512,512]{1,0:T(8,128)(2,1)} %copy-done.2, ...), custom_call_target="tpu_custom_call" | custom-call | flops 6600000000 | bytes 18000000 | tf_op jit(solution)/shard_map/project/pallas_call | solution.py:238
  81.7 3.3 %collective-permute-start.10 = (bf16[4,128,256]{2,1,0:T(8,128)(2,1)}, bf16[4,128,256]{2,1,0:T(8,128)(2,1)S(1)}, u32[]{:S(2)}, u32[]{:S(2)}) collective-permute-start(bf16[4,128,256]{2,1,0:T(8,128)(2,1)} %get-tuple-element.29), channel_id=1, source_target_pairs={{0,32},{4,36},{8,40},{12,44},{16,48},{20,52},{24,56},{28,60},{32,0... | collective-permute-start | bytes 786440 | tf_op jit(solution)/shard_map/ppermute | solution.py:424
  85.6 0.8 collective-permute-start.9
  86.4 5.0 %project.3 = (bf16[4,128,256]{2,1,0:T(8,128)(2,1)}, bf16[4,128,256]{2,1,0:T(8,128)(2,1)}, bf16[4,128,256]{2,1,0:T(8,128)(2,1)}, bf16[4,128,256]{2,1,0:T(8,128)(2,1)}) custom-call(s32[4]{0:T(128)} %pad_add_fusion.at_ref, bf16[512,512]{1,0:T(8,128)(2,1)} %bitcast.22, bf16[512,512]{1,0:T(8,128)(2,1)} %collective-permute-done.x1, bf16[512,512]{1,0:T(8,128)(2,1)} %copy-done.2, ...), custom_call_target="tpu_custom_call" | custom-call | flops 6600000000 | bytes 18000000 | tf_op jit(solution)/shard_map/project/pallas_call | solution.py:238
  91.9 2.5 collective-permute-start.17
  94.4 15.7 %collective-permute-done.10.m2 = bf16[4,128,256]{2,1,0:T(8,128)(2,1)S(1)} collective-permute-done((bf16[4,128,256]{2,1,0:T(8,128)(2,1)}, bf16[4,128,256]{2,1,0:T(8,128)(2,1)S(1)}, u32[]{:S(2)}, u32[]{:S(2)}) %collective-permute-start.10) | collective-permute-done | bytes 262176 | tf_op jit(solution)/shard_map/ppermute | solution.py:424
  110.4 3.2 %collective-permute-done.11.m3 = bf16[4,128,256]{2,1,0:T(8,128)(2,1)S(1)} collective-permute-done((bf16[4,128,256]{2,1,0:T(8,128)(2,1)}, bf16[4,128,256]{2,1,0:T(8,128)(2,1)S(1)}, u32[]{:S(2)}, u32[]{:S(2)}) %collective-permute-start.11) | collective-permute-done | bytes 262176 | tf_op jit(solution)/shard_map/ppermute | solution.py:424
  113.6 2.2 collective-permute-done.9.m1
  115.8 5.7 %collective-permute-done.16.o1 = bf16[4,128,256]{2,1,0:T(8,128)(2,1)S(1)} collective-permute-done((bf16[4,128,256]{2,1,0:T(8,128)(2,1)}, bf16[4,128,256]{2,1,0:T(8,128)(2,1)S(1)}, u32[]{:S(2)}, u32[]{:S(2)}) %collective-permute-start.16) | collective-permute-done | bytes 262176 | tf_op jit(solution)/shard_map/ppermute | solution.py:424
  121.4 5.5 %collective-permute-done.17.o2 = bf16[4,128,256]{2,1,0:T(8,128)(2,1)S(1)} collective-permute-done((bf16[4,128,256]{2,1,0:T(8,128)(2,1)}, bf16[4,128,256]{2,1,0:T(8,128)(2,1)S(1)}, u32[]{:S(2)}, u32[]{:S(2)}) %collective-permute-start.17) | collective-permute-done | bytes 262176 | tf_op jit(solution)/shard_map/ppermute | solution.py:424
  127.8 5.7 %sum_pack.1 = bf16[128,144,128]{2,1,0:T(8,128)(2,1)} custom-call(s32[4]{0:T(128)} %pad_add_fusion.at_ref, bf16[4,128,256]{2,1,0:T(8,128)(2,1)} %get-tuple-element.27.m0, bf16[4,128,256]{2,1,0:T(8,128)(2,1)} %copy-done.5, bf16[4,128,256]{2,1,0:T(8,128)(2,1)} %copy-done.3, bf16[4,128,256]{2,1,0:T(8,128)(2,1)} %copy-done.4, ...), custom_call_target="tpu_custom_call" | custom-call | flops 6049999872 | bytes 16500000 | tf_op jit(solution)/shard_map/sum_pack/pallas_call | solution.py:265
  133.4 8.7 %all-to-all-start = ((bf16[128,144,128]{2,1,0:T(8,128)(2,1)}), bf16[128,144,128]{2,1,0:T(8,128)(2,1)}, u32[]{:S(2)}, u32[]{:S(2)}) async-start(bf16[128,144,128]{2,1,0:T(8,128)(2,1)} %sum_pack.1), calls=%async_computation | async-start | bytes 9437184 | tf_op jit(solution)/shard_map/all_to_all | solution.py:391
  142.2 12.7 %gate_factors.1.fac_ref = bf16[1152,1536]{1,0:T(8,128)(2,1)} custom-call(bf16[128,72,128]{2,1,0:T(8,128)(2,1)} %copy-done, bf16[128,72,128]{2,1,0:T(8,128)(2,1)} %all-to-all-done.2.msg1, bf16[2048,1536]{1,0:T(8,128)(2,1)} %bitcast.12), custom_call_target="tpu_custom_call" | custom-call | flops 13749999616 | bytes 37500000 | tf_op jit(solution)/shard_map/gate_factors/pallas_call | solution.py:308
  154.8 50.2 %all-to-all-done.msg0.msg1 = bf16[128,144,128]{2,1,0:T(8,128)(2,1)} async-done(((bf16[128,144,128]{2,1,0:T(8,128)(2,1)}), bf16[128,144,128]{2,1,0:T(8,128)(2,1)}, u32[]{:S(2)}, u32[]{:S(2)}) %all-to-all-start) | async-done | bytes 4718624 | tf_op jit(solution)/shard_map/all_to_all | solution.py:391
  205.0 20.7 %expert_back.1 = bf16[128,144,128]{2,1,0:T(8,128)(2,1)} custom-call(bf16[128,144,128]{2,1,0:T(8,128)(2,1)} %all-to-all-done.msg0.msg1, bf16[128,144,128]{2,1,0:T(8,128)(2,1)} %all-to-all-done.msg0.msg1, bf16[1152,1536]{1,0:T(8,128)(2,1)} %gate_factors.1.fac_ref, bf16[768,2048]{1,0:T(8,128)(2,1)} %bitcast.14, bf16[2048,1536]{1,0:T(8,128)(2,1)} %bitcast.13), custom_call_target="tpu_custom_call" | custom-call | flops 22000001024 | bytes 60000000 | tf_op jit(solution)/shard_map/expert_back/pallas_call | solution.py:343
  225.7 7.0 %all-to-all-start.3 = ((bf16[128,144,128]{2,1,0:T(8,128)(2,1)}), bf16[128,144,128]{2,1,0:T(8,128)(2,1)}, u32[]{:S(2)}, u32[]{:S(2)}) async-start(bf16[128,144,128]{2,1,0:T(8,128)(2,1)} %expert_back.1), calls=%async_computation.3 | async-start | bytes 9437184 | tf_op jit(solution)/shard_map/all_to_all | solution.py:391
  232.7 2.2 combine_weights.1.w_ref
  234.9 60.6 %all-to-all-done.3.msg_ref = bf16[128,144,128]{2,1,0:T(8,128)(2,1)} async-done(((bf16[128,144,128]{2,1,0:T(8,128)(2,1)}), bf16[128,144,128]{2,1,0:T(8,128)(2,1)}, u32[]{:S(2)}, u32[]{:S(2)}) %all-to-all-start.3) | async-done | bytes 4718624 | tf_op jit(solution)/shard_map/all_to_all | solution.py:391
  295.5 5.3 %combine.1 = bf16[128,2048]{1,0:T(8,128)(2,1)} custom-call(bf16[128,144,128]{2,1,0:T(8,128)(2,1)} %all-to-all-done.3.msg_ref, bf16[256,1152]{1,0:T(8,128)(2,1)} %combine_weights.1.w_ref), custom_call_target="tpu_custom_call" | custom-call | flops 5830000128 | bytes 15900000 | tf_op jit(solution)/shard_map/combine/pallas_call | solution.py:374
  (49 shorter events, 5.7 us)
Async XLA Ops:
  0.9 37.5 %collective-permute-start.3 = (bf16[256,256]{1,0:T(8,128)(2,1)S(1)}, bf16[256,256]{1,0:T(8,128)(2,1)S(1)}, u32[]{:S(2)}, u32[]{:S(2)}) collective-permute-start(bf16[256,256]{1,0:T(8,128)(2,1)S(1)} %get-tuple-element.38), channel_id=1, source_target_pairs={{0,4},{4,8},{8,12},{12,0},{16,20},{20,24},{24,28},{28,16},{32,36},... | collective-permute-start | bytes 393224 | tf_op jit(solution)/shard_map/ppermute | solution.py:420
  2.0 36.4 %collective-permute-start.4 = (bf16[256,256]{1,0:T(8,128)(2,1)S(1)}, bf16[256,256]{1,0:T(8,128)(2,1)S(1)}, u32[]{:S(2)}, u32[]{:S(2)}) collective-permute-start(bf16[256,256]{1,0:T(8,128)(2,1)S(1)} %get-tuple-element.38), channel_id=1, source_target_pairs={{0,8},{4,12},{8,0},{12,4},{16,24},{20,28},{24,16},{28,20},{32,40},... | collective-permute-start | bytes 393224 | tf_op jit(solution)/shard_map/ppermute | solution.py:420
  2.3 36.1 %collective-permute-start.5 = (bf16[256,256]{1,0:T(8,128)(2,1)S(1)}, bf16[256,256]{1,0:T(8,128)(2,1)S(1)}, u32[]{:S(2)}, u32[]{:S(2)}) collective-permute-start(bf16[256,256]{1,0:T(8,128)(2,1)S(1)} %get-tuple-element.38), channel_id=1, source_target_pairs={{0,12},{4,0},{8,4},{12,8},{16,28},{20,16},{24,20},{28,24},{32,44},... | collective-permute-start | bytes 393224 | tf_op jit(solution)/shard_map/ppermute | solution.py:420
  7.6 49.0 %all-to-all-start.1 = ((bf16[128,72,128]{2,1,0:T(8,128)(2,1)}), bf16[128,72,128]{2,1,0:T(8,128)(2,1)S(1)}, u32[]{:S(2)}, u32[]{:S(2)}) async-start(bf16[128,72,128]{2,1,0:T(8,128)(2,1)} %get-tuple-element.35), calls=%async_computation.1 | async-start | bytes 4718592 | tf_op jit(solution)/shard_map/all_to_all | solution.py:391
  35.8 20.8 %collective-permute-start = (bf16[512,512]{1,0:T(8,128)(2,1)}, bf16[512,512]{1,0:T(8,128)(2,1)}, u32[]{:S(2)}, u32[]{:S(2)}) collective-permute-start(bf16[512,512]{1,0:T(8,128)(2,1)} %bitcast.17), channel_id=1, source_target_pairs={{0,4},{4,8},{8,12},{12,0},{16,20},{20,24},{24,28},{28,16},{32,36},... | collective-permute-start | bytes 1572872 | tf_op jit(solution)/shard_map/ppermute | solution.py:420
  38.5 38.2 %copy-start.1 = (bf16[1280,256]{1,0:T(8,128)(2,1)}, bf16[1280,256]{1,0:T(8,128)(2,1)S(1)}, u32[]{:S(2)}) copy-start(bf16[1280,256]{1,0:T(8,128)(2,1)S(1)} %maximum_dynamic-update-slice_fusion.w0) | copy-start | bytes 1966084
  38.5 37.5 %collective-permute-start.6 = (bf16[1280,256]{1,0:T(8,128)(2,1)S(1)}, bf16[1280,256]{1,0:T(8,128)(2,1)}, u32[]{:S(2)}, u32[]{:S(2)}) collective-permute-start(bf16[1280,256]{1,0:T(8,128)(2,1)S(1)} %maximum_dynamic-update-slice_fusion.w0), channel_id=1, source_target_pairs={{0,1},{1,2},{2,3},{3,0},{4,5},{5,6},{6,7},{7,4},{8,9},{9,10},{10,1... | collective-permute-start | bytes 1966088 | tf_op jit(solution)/shard_map/ppermute | solution.py:427
  39.8 36.4 %collective-permute-start.7 = (bf16[1280,256]{1,0:T(8,128)(2,1)S(1)}, bf16[1280,256]{1,0:T(8,128)(2,1)}, u32[]{:S(2)}, u32[]{:S(2)}) collective-permute-start(bf16[1280,256]{1,0:T(8,128)(2,1)S(1)} %maximum_dynamic-update-slice_fusion.w0), channel_id=1, source_target_pairs={{0,2},{1,3},{2,0},{3,1},{4,6},{5,7},{6,4},{7,5},{8,10},{9,11},{10,... | collective-permute-start | bytes 1966088 | tf_op jit(solution)/shard_map/ppermute | solution.py:427
  40.6 35.9 %collective-permute-start.8 = (bf16[1280,256]{1,0:T(8,128)(2,1)S(1)}, bf16[1280,256]{1,0:T(8,128)(2,1)}, u32[]{:S(2)}, u32[]{:S(2)}) collective-permute-start(bf16[1280,256]{1,0:T(8,128)(2,1)S(1)} %maximum_dynamic-update-slice_fusion.w0), channel_id=1, source_target_pairs={{0,3},{1,0},{2,1},{3,2},{4,7},{5,4},{6,5},{7,6},{8,11},{9,8},{10,9... | collective-permute-start | bytes 1966088 | tf_op jit(solution)/shard_map/ppermute | solution.py:427
  42.5 33.1 %collective-permute-start.1 = (bf16[512,512]{1,0:T(8,128)(2,1)}, bf16[512,512]{1,0:T(8,128)(2,1)S(1)}, u32[]{:S(2)}, u32[]{:S(2)}) collective-permute-start(bf16[512,512]{1,0:T(8,128)(2,1)} %bitcast.16), channel_id=1, source_target_pairs={{0,8},{4,12},{8,0},{12,4},{16,24},{20,28},{24,16},{28,20},{32,40},... | collective-permute-start | bytes 1572872 | tf_op jit(solution)/shard_map/ppermute | solution.py:420
  56.6 20.1 %collective-permute-start.2 = (bf16[512,512]{1,0:T(8,128)(2,1)}, bf16[512,512]{1,0:T(8,128)(2,1)}, u32[]{:S(2)}, u32[]{:S(2)}) collective-permute-start(bf16[512,512]{1,0:T(8,128)(2,1)} %bitcast.15), channel_id=1, source_target_pairs={{0,12},{4,0},{8,4},{12,8},{16,28},{20,16},{24,20},{28,24},{32,44},... | collective-permute-start | bytes 1572872 | tf_op jit(solution)/shard_map/ppermute | solution.py:420
  56.7 25.0 %copy-start = (bf16[128,72,128]{2,1,0:T(8,128)(2,1)}, bf16[128,72,128]{2,1,0:T(8,128)(2,1)S(1)}, u32[]{:S(2)}) copy-start(bf16[128,72,128]{2,1,0:T(8,128)(2,1)S(1)} %all-to-all-done.1.msg0) | copy-start | bytes 7077892
  56.7 76.8 %all-to-all-start.2 = ((bf16[128,72,128]{2,1,0:T(8,128)(2,1)}), bf16[128,72,128]{2,1,0:T(8,128)(2,1)}, u32[]{:S(2)}, u32[]{:S(2)}) async-start(bf16[128,72,128]{2,1,0:T(8,128)(2,1)} %get-tuple-element.36), calls=%async_computation.2 | async-start | bytes 4718592 | tf_op jit(solution)/shard_map/all_to_all | solution.py:391
  75.5 1.1 copy-start.2
  75.6 9.4 %collective-permute-start.12 = (bf16[1280,256]{1,0:T(8,128)(2,1)S(1)}, bf16[1280,256]{1,0:T(8,128)(2,1)}, u32[]{:S(2)}, u32[]{:S(2)}) collective-permute-start(bf16[1280,256]{1,0:T(8,128)(2,1)S(1)} %maximum_dynamic-update-slice_fusion.w0), channel_id=1, source_target_pairs={{0,64},{64,0},{1,65},{65,1},{2,66},{66,2},{3,67},{67,3},{4,68},{68... | collective-permute-start | bytes 1966088 | tf_op jit(solution)/shard_map/ppermute | solution.py:437
  76.0 9.6 %collective-permute-start.13 = (bf16[1280,256]{1,0:T(8,128)(2,1)}, bf16[1280,256]{1,0:T(8,128)(2,1)}, u32[]{:S(2)}, u32[]{:S(2)}) collective-permute-start(bf16[1280,256]{1,0:T(8,128)(2,1)} %collective-permute-done.6.w1), channel_id=1, source_target_pairs={{0,64},{64,0},{1,65},{65,1},{2,66},{66,2},{3,67},{67,3},{4,68},{68... | collective-permute-start | bytes 1966088 | tf_op jit(solution)/shard_map/ppermute | solution.py:437
  76.2 10.3 %collective-permute-start.14 = (bf16[1280,256]{1,0:T(8,128)(2,1)}, bf16[1280,256]{1,0:T(8,128)(2,1)}, u32[]{:S(2)}, u32[]{:S(2)}) collective-permute-start(bf16[1280,256]{1,0:T(8,128)(2,1)} %collective-permute-done.7.w2), channel_id=1, source_target_pairs={{0,64},{64,0},{1,65},{65,1},{2,66},{66,2},{3,67},{67,3},{4,68},{68... | collective-permute-start | bytes 1966088 | tf_op jit(solution)/shard_map/ppermute | solution.py:437
  76.5 9.9 %collective-permute-start.15 = (bf16[1280,256]{1,0:T(8,128)(2,1)}, bf16[1280,256]{1,0:T(8,128)(2,1)}, u32[]{:S(2)}, u32[]{:S(2)}) collective-permute-start(bf16[1280,256]{1,0:T(8,128)(2,1)} %collective-permute-done.8.w3), channel_id=1, source_target_pairs={{0,64},{64,0},{1,65},{65,1},{2,66},{66,2},{3,67},{67,3},{4,68},{68... | collective-permute-start | bytes 1966088 | tf_op jit(solution)/shard_map/ppermute | solution.py:437
  81.7 28.4 %collective-permute-start.10 = (bf16[4,128,256]{2,1,0:T(8,128)(2,1)}, bf16[4,128,256]{2,1,0:T(8,128)(2,1)S(1)}, u32[]{:S(2)}, u32[]{:S(2)}) collective-permute-start(bf16[4,128,256]{2,1,0:T(8,128)(2,1)} %get-tuple-element.29), channel_id=1, source_target_pairs={{0,32},{4,36},{8,40},{12,44},{16,48},{20,52},{24,56},{28,60},{32,0... | collective-permute-start | bytes 786440 | tf_op jit(solution)/shard_map/ppermute | solution.py:424
  84.9 28.6 %collective-permute-start.11 = (bf16[4,128,256]{2,1,0:T(8,128)(2,1)}, bf16[4,128,256]{2,1,0:T(8,128)(2,1)S(1)}, u32[]{:S(2)}, u32[]{:S(2)}) collective-permute-start(bf16[4,128,256]{2,1,0:T(8,128)(2,1)} %get-tuple-element.30), channel_id=1, source_target_pairs={{0,48},{4,52},{8,56},{12,60},{16,0},{20,4},{24,8},{28,12},{32,16},... | collective-permute-start | bytes 786440 | tf_op jit(solution)/shard_map/ppermute | solution.py:424
  85.6 30.2 %collective-permute-start.9 = (bf16[4,128,256]{2,1,0:T(8,128)(2,1)}, bf16[4,128,256]{2,1,0:T(8,128)(2,1)S(1)}, u32[]{:S(2)}, u32[]{:S(2)}) collective-permute-start(bf16[4,128,256]{2,1,0:T(8,128)(2,1)} %get-tuple-element.28), channel_id=1, source_target_pairs={{0,16},{4,20},{8,24},{12,28},{16,32},{20,36},{24,40},{28,44},{32,4... | collective-permute-start | bytes 786440 | tf_op jit(solution)/shard_map/ppermute | solution.py:424
  91.4 30.1 %collective-permute-start.16 = (bf16[4,128,256]{2,1,0:T(8,128)(2,1)}, bf16[4,128,256]{2,1,0:T(8,128)(2,1)S(1)}, u32[]{:S(2)}, u32[]{:S(2)}) collective-permute-start(bf16[4,128,256]{2,1,0:T(8,128)(2,1)} %get-tuple-element.32), channel_id=1, source_target_pairs={{0,16},{4,20},{8,24},{12,28},{16,32},{20,36},{24,40},{28,44},{32,4... | collective-permute-start | bytes 786440 | tf_op jit(solution)/shard_map/ppermute | solution.py:424
  91.9 35.0 %collective-permute-start.17 = (bf16[4,128,256]{2,1,0:T(8,128)(2,1)}, bf16[4,128,256]{2,1,0:T(8,128)(2,1)S(1)}, u32[]{:S(2)}, u32[]{:S(2)}) collective-permute-start(bf16[4,128,256]{2,1,0:T(8,128)(2,1)} %get-tuple-element.33), channel_id=1, source_target_pairs={{0,32},{4,36},{8,40},{12,44},{16,48},{20,52},{24,56},{28,60},{32,0... | collective-permute-start | bytes 786440 | tf_op jit(solution)/shard_map/ppermute | solution.py:424
  110.1 16.9 %copy-start.3 = (bf16[4,128,256]{2,1,0:T(8,128)(2,1)}, bf16[4,128,256]{2,1,0:T(8,128)(2,1)S(1)}, u32[]{:S(2)}) copy-start(bf16[4,128,256]{2,1,0:T(8,128)(2,1)S(1)} %collective-permute-done.10.m2) | copy-start | bytes 786436
  110.1 16.9 %collective-permute-start.18 = (bf16[4,128,256]{2,1,0:T(8,128)(2,1)}, bf16[4,128,256]{2,1,0:T(8,128)(2,1)S(1)}, u32[]{:S(2)}, u32[]{:S(2)}) collective-permute-start(bf16[4,128,256]{2,1,0:T(8,128)(2,1)} %get-tuple-element.34), channel_id=1, source_target_pairs={{0,48},{4,52},{8,56},{12,60},{16,0},{20,4},{24,8},{28,12},{32,16},... | collective-permute-start | bytes 786440 | tf_op jit(solution)/shard_map/ppermute | solution.py:424
  113.6 13.4 %copy-start.4 = (bf16[4,128,256]{2,1,0:T(8,128)(2,1)}, bf16[4,128,256]{2,1,0:T(8,128)(2,1)S(1)}, u32[]{:S(2)}) copy-start(bf16[4,128,256]{2,1,0:T(8,128)(2,1)S(1)} %collective-permute-done.11.m3) | copy-start | bytes 786436
  115.8 11.2 %copy-start.5 = (bf16[4,128,256]{2,1,0:T(8,128)(2,1)}, bf16[4,128,256]{2,1,0:T(8,128)(2,1)S(1)}, u32[]{:S(2)}) copy-start(bf16[4,128,256]{2,1,0:T(8,128)(2,1)S(1)} %collective-permute-done.9.m1) | copy-start | bytes 786436
  121.4 5.6 %copy-start.6 = (bf16[4,128,256]{2,1,0:T(8,128)(2,1)}, bf16[4,128,256]{2,1,0:T(8,128)(2,1)S(1)}, u32[]{:S(2)}) copy-start(bf16[4,128,256]{2,1,0:T(8,128)(2,1)S(1)} %collective-permute-done.16.o1) | copy-start | bytes 786436
  127.0 0.7 copy-start.7
  127.0 0.8 copy-start.8
  133.4 71.6 %all-to-all-start = ((bf16[128,144,128]{2,1,0:T(8,128)(2,1)}), bf16[128,144,128]{2,1,0:T(8,128)(2,1)}, u32[]{:S(2)}, u32[]{:S(2)}) async-start(bf16[128,144,128]{2,1,0:T(8,128)(2,1)} %sum_pack.1), calls=%async_computation | async-start | bytes 9437184 | tf_op jit(solution)/shard_map/all_to_all | solution.py:391
  225.7 69.9 %all-to-all-start.3 = ((bf16[128,144,128]{2,1,0:T(8,128)(2,1)}), bf16[128,144,128]{2,1,0:T(8,128)(2,1)}, u32[]{:S(2)}, u32[]{:S(2)}) async-start(bf16[128,144,128]{2,1,0:T(8,128)(2,1)} %expert_back.1), calls=%async_computation.3 | async-start | bytes 9437184 | tf_op jit(solution)/shard_map/all_to_all | solution.py:391

commit v3 on v2

--- a/solution.py
+++ b/solution.py
@@ -213,72 +213,90 @@
     )(place, queries, out_grad, keys, values)
 
 
-def project_kernel(at_ref, x0, x1, x2, x3, w0, w1, w2, w3, out0, out1, out2, out3, scr):
+def project_kernel(at_ref, x0, x1, x2, x3, *refs):
+    *weights, out0, out1, out2, out3, scr = refs
     pieces = (x0, x1, x2, x3)
     total = x0[:, 2 * HD :].astype(F32)
     for x in pieces[1:]:
         total = total + x[:, 2 * HD :].astype(F32)
     total = total.astype(BF)
     width = scr.shape[3]
-    for k, w_ref in enumerate((w0, w1, w2, w3)):
-        acc = dot_nt(total, w_ref[N_Y * width :])
-        for y, x in enumerate(pieces):
-            acc = acc + dot_nt(x[:, : 2 * HD], w_ref[y * width : (y + 1) * width])
-        col = jnp.bitwise_and(at_ref[3] - k, 3)
-        for z in range(N_Z):
-            scr[z, col] = acc[z * TOK : (z + 1) * TOK].astype(BF)
+    unit = 0
+    for w_ref in weights:
+        for h in range(w_ref.shape[0]):
+            acc = dot_nt(total, w_ref[h, N_Y * width :])
+            for y, x in enumerate(pieces):
+                acc = acc + dot_nt(x[:, : 2 * HD], w_ref[h, y * width : (y + 1) * width])
+            for z in range(N_Z):
+                scr[z, unit] = acc[z * TOK : (z + 1) * TOK].astype(BF)
+            unit += 1
     for k, out in enumerate((out0, out1, out2, out3)):
         out[...] = scr[jnp.bitwise_and(at_ref[0] + k, N_Z - 1)]
 
 
 def project(place, pieces, weights):
-    width = weights[0].shape[0] // (N_Y + 1)
-    out = jax.ShapeDtypeStruct((len(weights), TOK, width), BF)
+    width = weights[0].shape[1] // (N_Y + 1)
+    units = sum(w.shape[0] for w in weights)
     whole = pl.BlockSpec(memory_space=pltpu.VMEM)
     return pl.pallas_call(
         project_kernel,
-        in_specs=[pl.BlockSpec(memory_space=pltpu.SMEM)] + [whole] * 8,
+        in_specs=[pl.BlockSpec(memory_space=pltpu.SMEM)] + [whole] * (N_Y + len(weights)),
         out_specs=[whole] * N_Z,
-        out_shape=[out] * N_Z,
-        scratch_shapes=[pltpu.VMEM((N_Z, len(weights), TOK, width), BF)],
+        out_shape=[jax.ShapeDtypeStruct((units, TOK, width), BF)] * N_Z,
+        scratch_shapes=[pltpu.VMEM((N_Z, units, TOK, width), BF)],
         compiler_params=pltpu.CompilerParams(vmem_limit_bytes=VMEM_LIMIT),
         name="project",
-        cost_estimate=cost(6),
+        cost_estimate=cost(0.6 * units),
     )(place, *pieces, *weights)
 
 
-def sum_pack_kernel(at_ref, m0, m1, m2, m3, o0, o1, o2, o3, resid_ref, pick_ref, out_ref, scr):
+def sum_pack_kernel(at_ref, m0, m1, m2, m3, o0, o1, o2, o3, resid_ref, pick_ref, out_ref, sums, scr):
+    @pl.when(pl.program_id(0) == 0)
+    def _():
+        mine = m0.shape[0]
+        for u in range(mine):
+            sums[u] = sum((x[u].astype(F32) for x in (m1, m2, m3)), m0[u].astype(F32))
+        for u in range(o0.shape[0]):
+            sums[mine + u] = sum((x[u].astype(F32) for x in (o1, o2, o3)), o0[u].astype(F32))
+
+    section, col = at_ref[2], at_ref[3]
     blocks = []
     for c in range(2):
-        mine, other = (
-            sum((x[c].astype(F32) for x in xs[1:]), xs[0][c].astype(F32))
-            for xs in ((m0, m1, m2, m3), (o0, o1, o2, o3))
-        )
+        behind = jnp.bitwise_and(2 * pl.program_id(0) + c - col, 3)
         for h in range(2):
-            blocks.append(jnp.where(at_ref[2] == h, mine, other))
+            far = jnp.where(section == h, 4, 7)
+            near = jnp.where(behind == jnp.where(section == 0, 3, 1), 2 + h, 5 + h)
+            unit = jnp.where(behind == 0, h, jnp.where(behind == 2, far, near))
+            blocks.append(sums[unit])
     total = resid_ref[...].astype(F32) + jnp.concatenate(blocks, axis=1)
     pack_half(total.astype(BF), pick_ref[...], out_ref, scr)
 
 
 def sum_pack(place, mine, other, resid, pick):
-    part = pl.BlockSpec((2, TOK, 256), lambda n, at: (n, 0, 0))
+    def whole(x):
+        return pl.BlockSpec(x.shape, lambda n, at: (0, 0, 0))
+
+    units = mine[0].shape[0] + other[0].shape[0]
     return pl.pallas_call(
         sum_pack_kernel,
         grid_spec=pltpu.PrefetchScalarGridSpec(
             num_scalar_prefetch=1,
             grid=(2,),
-            in_specs=[part] * 8
+            in_specs=[whole(x) for x in (*mine, *other)]
             + [
                 pl.BlockSpec((TOK, HALF), lambda n, at: (0, n)),
                 pl.BlockSpec((NE * CAP, TOK), lambda n, at: (0, 0)),
             ],
             out_specs=pl.BlockSpec((NE, MSG, 128), lambda n, at: (0, n, 0)),
-            scratch_shapes=[pltpu.VMEM((NE * 8, 128), F32)],
+            scratch_shapes=[
+                pltpu.VMEM((units, TOK, 256), F32),
+                pltpu.VMEM((NE * 8, 128), F32),
+            ],
         ),
         out_shape=jax.ShapeDtypeStruct((NE, 2 * MSG, 128), BF),
         compiler_params=params(1),
         name="sum_pack",
-        cost_estimate=cost(5.5),
+        cost_estimate=cost(4),
     )(place, *mine, *other, resid, pick)
 
 
@@ -423,18 +441,28 @@
         hops = [(N_Y * z + y, N_Y * ((z + k) % N_Z) + y) for z in range(N_Z) for y in range(N_Y)]
         return lax.ppermute(x, "row", hops)
 
-    def ahead_c(x, k):
-        return lax.ppermute(x, "col", [(c, (c + k) % n_col) for c in range(n_col)])
-
     half = D // n_col // 2
-    wq = lax.dynamic_slice_in_dim(q_weight, section * half, half, 0)
-    wk = lax.dynamic_slice(k_weight, (section * half, kv_index * HD), (half, HD))
-    wv = lax.dynamic_slice(v_weight, (section * half, kv_index * HD), (half, HD))
+    wk = lax.dynamic_slice_in_dim(k_weight, kv_index * HD, HD, 1)
+    wv = lax.dynamic_slice_in_dim(v_weight, kv_index * HD, HD, 1)
     w_own = jnp.concatenate(
-        [wq, *(ahead_y(wq, k) for k in others), jnp.concatenate([wk, wv], axis=1)], axis=0
+        [
+            w.reshape(2, half, 2 * HD)
+            for w in (
+                q_weight,
+                *(ahead_y(q_weight, k) for k in others),
+                jnp.concatenate([wk, wv], axis=1),
+            )
+        ],
+        axis=1,
     )
-    w_mine = [w_own] + [ahead_c(w_own, k) for k in others]
-    w_other = [lax.ppermute(w, "section", [(0, 1), (1, 0)]) for w in w_mine]
+    near_hops = [(c, (c + 1) % n_col) for c in range(n_col)]
+    near_hops += [(n_col + c, n_col + (c - 1) % n_col) for c in range(n_col)]
+    w_near = lax.ppermute(w_own, ("section", "col"), near_hops)
+    w_far = lax.ppermute(
+        lax.dynamic_slice_in_dim(w_own, section, 1, 0),
+        "col",
+        [(c, (c + 2) % n_col) for c in range(n_col)],
+    )
 
     ids_t = expert_ids.T
     pick, *send_rows = route_pack(ids_t, moe_input)
@@ -445,6 +473,11 @@
     pieces = attention(place, queries, out_grad, keys, values)
     pieces = [p.reshape(N_Z * TOK, 4 * HD) for p in pieces]
     pieces = [pieces[0]] + [ahead_y(pieces[k], k) for k in others]
+
+    w_near, w_far, *pieces = lax.optimization_barrier((w_near, w_far, *pieces))
+    swap = [(0, 1), (1, 0)]
+    w_mine = [w_own, w_near, w_far]
+    w_other = [lax.ppermute(w_near, "section", swap), lax.ppermute(w_far, "section", swap)]
 
     def head_half(weights):
         parts = project(place, pieces, weights)

time: 302 us -> 298 us (0.987)
  starting transfers between devices: 63.1 us -> 51 us
  local copies, waits for them, and re-layouts: 3.44 us -> 10.8 us
    ppermute x6, waiting for transfers between devices: 32.3 us -> 17.7 us  [ahead_z(): return lax.ppermute(x, 'row', hops)]
    all_to_all x4, starting transfers between devices: 46.2 us -> 35.8 us  [exchange(): lax.all_to_all(x, axis, split_axis=0, concat_axis=0, tiled=True, axis_ind...]
    ppermute x7 -> x4, waiting for transfers between devices: 0.02 us -> 10.3 us  [the longest x1 10.3 us: body(): lax.ppermute(lax.dynamic_slice_in_dim(w_own, section, 1, 0), 'col', [(c,...]
    unnamed x22 -> x26, local copies, waits for them, and re-layouts: 1.75 us -> 7.9 us
    ppermute x6, waiting for transfers between devices: 13.6 us -> 16.8 us  [ahead_y(): return lax.ppermute(x, 'row', hops)]
  transfers between devices with their start and end apart: 23 -> 20, of which waited for: 8 -> 10; matrix products, arithmetic and copies ran while one was open for 1% -> 3% of each run, Pallas kernels for 17% -> 17%
where the time goes in v3:
time: 298 us; the launch traced here: 297 us
  waiting for transfers between devices  158 us (53%)
  Pallas kernels  76.9 us (26%)
  starting transfers between devices  51 us (17%)
  local copies, waits for them, and re-layouts  10.8 us (4%)
    all_to_all x4, waiting for transfers between devices, exchange(): lax.all_to_all(x, axis, split_axis=0, concat_axis=0, tiled=True, axis_ind...  113 us
    all_to_all x4, starting transfers between devices, exchange(): lax.all_to_all(x, axis, split_axis=0, concat_axis=0, tiled=True, axis_ind...  35.8 us
    pallas_call x1, Pallas kernels, expert_back(): pl.pallas_call(expert_kernel, grid=(steps,), in_specs=[pl.BlockSpec((CHUN...  20.7 us
    ppermute x6, waiting for transfers between devices, ahead_z(): return lax.ppermute(x, 'row', hops)  17.7 us
    ppermute x6, waiting for transfers between devices, ahead_y(): return lax.ppermute(x, 'row', hops)  16.8 us
    pallas_call x1, Pallas kernels, attention(): pl.pallas_call(attention_kernel, grid_spec=pltpu.PrefetchScalarGridSpec(n...  15.9 us
    pallas_call x1, Pallas kernels, gate_factors(): pl.pallas_call(gate_up_kernel, grid=(steps,), in_specs=[pl.BlockSpec((CHU...  12.7 us
    ppermute x1, waiting for transfers between devices, body(): lax.ppermute(lax.dynamic_slice_in_dim(w_own, section, 1, 0), 'col', [(c,...  10.3 us
  transfers between devices with their start and end apart: 20, of which 10 were waited for; matrix products, arithmetic and copies ran while one was open for 3% of the time, Pallas kernels for 17%

profile of v3, /device:TPU:19, one launch (start us, length us, event | category | flops | bytes accessed | tf_op | source)
XLA Modules:
  0.0 297.0 jit_solution(4783268582316345692)
XLA Ops:
  0.0 1.0 collective-permute-start
  1.5 1.3 collective-permute-start.1
  2.8 4.4 %route_pack.1 = (bf16[1152,128]{1,0:T(8,128)(2,1)}, bf16[128,72,128]{2,1,0:T(8,128)(2,1)}, bf16[128,72,128]{2,1,0:T(8,128)(2,1)}) custom-call(s32[8,128]{1,0:T(8,128)} %bitcast.27, bf16[128,2048]{1,0:T(8,128)(2,1)} %x_ref.1), custom_call_target="tpu_custom_call" | custom-call | flops 5500000256 | bytes 15000000 | tf_op jit(solution)/shard_map/route_pack/pallas_call | solution.py:102
  7.2 11.4 %all-to-all-start.1 = ((bf16[128,72,128]{2,1,0:T(8,128)(2,1)}), bf16[128,72,128]{2,1,0:T(8,128)(2,1)S(1)}, u32[]{:S(2)}, u32[]{:S(2)}) async-start(bf16[128,72,128]{2,1,0:T(8,128)(2,1)} %get-tuple-element.47), calls=%async_computation.1 | async-start | bytes 4718592 | tf_op jit(solution)/shard_map/all_to_all | solution.py:409
  21.8 1.7 constant_dynamic-update-slice_fusion.2
  25.2 1.2 constant_dynamic-slice_fusion
  26.4 2.2 collective-permute-start.4
  28.5 15.9 %attention.1 = (bf16[4,128,512]{2,1,0:T(8,128)(2,1)}, bf16[4,128,512]{2,1,0:T(8,128)(2,1)}, bf16[4,128,512]{2,1,0:T(8,128)(2,1)}, bf16[4,128,512]{2,1,0:T(8,128)(2,1)}) custom-call(s32[4]{0:T(128)} %pad_add_fusion.at_ref, bf16[2048,256]{1,0:T(8,128)(2,1)} %q_ref, bf16[2048,256]{1,0:T(8,128)(2,1)} %g_ref.1, bf16[2048,512]{1,0:T(8,128)(2,1)} %k_ref.1, ...), custom_call_target="tpu_custom_call" | custom-call | flops 17600000000 | bytes 48000000 | tf_op jit(solution)/shard_map/attention/pallas_call | solution.py:196
  46.8 1.9 all-to-all-done.1.msg0
  48.7 1.4 copy-done
  50.1 9.4 %all-to-all-start.2 = ((bf16[128,72,128]{2,1,0:T(8,128)(2,1)}), bf16[128,72,128]{2,1,0:T(8,128)(2,1)}, u32[]{:S(2)}, u32[]{:S(2)}) async-start(bf16[128,72,128]{2,1,0:T(8,128)(2,1)} %get-tuple-element.48), calls=%async_computation.2 | async-start | bytes 4718592 | tf_op jit(solution)/shard_map/all_to_all | solution.py:409
  59.6 14.7 %collective-permute-done.6.x2 = bf16[512,512]{1,0:T(8,128)(2,1)} collective-permute-done((bf16[512,512]{1,0:T(8,128)(2,1)}, bf16[512,512]{1,0:T(8,128)(2,1)}, u32[]{:S(2)}, u32[]{:S(2)}) %collective-permute-start.6) | collective-permute-done | bytes 524320 | tf_op jit(solution)/shard_map/ppermute | solution.py:438
  74.2 2.1 collective-permute-done.7.x3
  76.3 10.3 %collective-permute-done.4.refs_2_ = bf16[1,1280,256]{2,1,0:T(8,128)(2,1)} collective-permute-done((bf16[1,1280,256]{2,1,0:T(8,128)(2,1)S(1)}, bf16[1,1280,256]{2,1,0:T(8,128)(2,1)}, u32[]{:S(2)}, u32[]{:S(2)}) %collective-permute-start.4) | collective-permute-done | bytes 655392 | tf_op jit(solution)/shard_map/ppermute | solution.py:461
  87.1 5.6 %project.2 = (bf16[5,128,256]{2,1,0:T(8,128)(2,1)}, bf16[5,128,256]{2,1,0:T(8,128)(2,1)}, bf16[5,128,256]{2,1,0:T(8,128)(2,1)}, bf16[5,128,256]{2,1,0:T(8,128)(2,1)}) custom-call(s32[4]{0:T(128)} %pad_add_fusion.at_ref, bf16[512,512]{1,0:T(8,128)(2,1)} %bitcast.30, bf16[512,512]{1,0:T(8,128)(2,1)} %copy-done.4, bf16[512,512]{1,0:T(8,128)(2,1)} %collective-permute-done.6.x2, ...), custom_call_target="tpu_custom_call" | custom-call | flops 3300000000 | bytes 9000000 | tf_op jit(solution)/shard_map/project/pallas_call | solution.py:241
  92.7 1.5 collective-permute-start.8
  94.2 2.9 collective-permute-start.9
  98.9 1.1 copy-done.2
  99.9 4.3 %project.3 = (bf16[3,128,256]{2,1,0:T(8,128)(2,1)}, bf16[3,128,256]{2,1,0:T(8,128)(2,1)}, bf16[3,128,256]{2,1,0:T(8,128)(2,1)}, bf16[3,128,256]{2,1,0:T(8,128)(2,1)}) custom-call(s32[4]{0:T(128)} %pad_add_fusion.at_ref, bf16[512,512]{1,0:T(8,128)(2,1)} %bitcast.31, bf16[512,512]{1,0:T(8,128)(2,1)} %copy-done.4, bf16[512,512]{1,0:T(8,128)(2,1)} %collective-permute-done.6.x2, ...), custom_call_target="tpu_custom_call" | custom-call | flops 1980000000 | bytes 5399999 | tf_op jit(solution)/shard_map/project/pallas_call | solution.py:241
  105.4 2.5 collective-permute-done.8.m1
  108.5 6.8 %collective-permute-done.9.m2 = bf16[5,128,256]{2,1,0:T(8,128)(2,1)S(1)} collective-permute-done((bf16[5,128,256]{2,1,0:T(8,128)(2,1)}, bf16[5,128,256]{2,1,0:T(8,128)(2,1)S(1)}, u32[]{:S(2)}, u32[]{:S(2)}) %collective-permute-start.9) | collective-permute-done | bytes 327712 | tf_op jit(solution)/shard_map/ppermute | solution.py:442
  115.3 4.1 %collective-permute-done.13.o1 = bf16[3,128,256]{2,1,0:T(8,128)(2,1)S(1)} collective-permute-done((bf16[3,128,256]{2,1,0:T(8,128)(2,1)}, bf16[3,128,256]{2,1,0:T(8,128)(2,1)S(1)}, u32[]{:S(2)}, u32[]{:S(2)}) %collective-permute-start.13) | collective-permute-done | bytes 196640 | tf_op jit(solution)/shard_map/ppermute | solution.py:442
  119.4 4.3 %collective-permute-done.14.o2 = bf16[3,128,256]{2,1,0:T(8,128)(2,1)S(1)} collective-permute-done((bf16[3,128,256]{2,1,0:T(8,128)(2,1)}, bf16[3,128,256]{2,1,0:T(8,128)(2,1)S(1)}, u32[]{:S(2)}, u32[]{:S(2)}) %collective-permute-start.14) | collective-permute-done | bytes 196640 | tf_op jit(solution)/shard_map/ppermute | solution.py:442
  124.5 5.8 %sum_pack.1 = bf16[128,144,128]{2,1,0:T(8,128)(2,1)} custom-call(s32[4]{0:T(128)} %pad_add_fusion.at_ref, bf16[5,128,256]{2,1,0:T(8,128)(2,1)} %get-tuple-element.39.m0, bf16[5,128,256]{2,1,0:T(8,128)(2,1)} %copy-done.5, bf16[5,128,256]{2,1,0:T(8,128)(2,1)} %copy-done.6, bf16[5,128,256]{2,1,0:T(8,128)(2,1)} %copy-done.7, ...), custom_call_target="tpu_custom_call" | custom-call | flops 4400000000 | bytes 12000000 | tf_op jit(solution)/shard_map/sum_pack/pallas_call | solution.py:280
  130.3 7.6 %all-to-all-start = ((bf16[128,144,128]{2,1,0:T(8,128)(2,1)}), bf16[128,144,128]{2,1,0:T(8,128)(2,1)}, u32[]{:S(2)}, u32[]{:S(2)}) async-start(bf16[128,144,128]{2,1,0:T(8,128)(2,1)} %sum_pack.1), calls=%async_computation | async-start | bytes 9437184 | tf_op jit(solution)/shard_map/all_to_all | solution.py:409
  138.0 12.7 %gate_factors.1.fac_ref = bf16[1152,1536]{1,0:T(8,128)(2,1)} custom-call(bf16[128,72,128]{2,1,0:T(8,128)(2,1)} %copy-done, bf16[128,72,128]{2,1,0:T(8,128)(2,1)} %all-to-all-done.2.msg1, bf16[2048,1536]{1,0:T(8,128)(2,1)} %bitcast.21), custom_call_target="tpu_custom_call" | custom-call | flops 13749999616 | bytes 37500000 | tf_op jit(solution)/shard_map/gate_factors/pallas_call | solution.py:326
  150.6 50.2 %all-to-all-done.msg0.msg1 = bf16[128,144,128]{2,1,0:T(8,128)(2,1)} async-done(((bf16[128,144,128]{2,1,0:T(8,128)(2,1)}), bf16[128,144,128]{2,1,0:T(8,128)(2,1)}, u32[]{:S(2)}, u32[]{:S(2)}) %all-to-all-start) | async-done | bytes 4718624 | tf_op jit(solution)/shard_map/all_to_all | solution.py:409
  200.8 20.7 %expert_back.1 = bf16[128,144,128]{2,1,0:T(8,128)(2,1)} custom-call(bf16[128,144,128]{2,1,0:T(8,128)(2,1)} %all-to-all-done.msg0.msg1, bf16[128,144,128]{2,1,0:T(8,128)(2,1)} %all-to-all-done.msg0.msg1, bf16[1152,1536]{1,0:T(8,128)(2,1)} %gate_factors.1.fac_ref, bf16[768,2048]{1,0:T(8,128)(2,1)} %bitcast.23, bf16[2048,1536]{1,0:T(8,128)(2,1)} %bitcast.22), custom_call_target="tpu_custom_call" | custom-call | flops 22000001024 | bytes 60000000 | tf_op jit(solution)/shard_map/expert_back/pallas_call | solution.py:361
  221.5 7.3 %all-to-all-start.3 = ((bf16[128,144,128]{2,1,0:T(8,128)(2,1)}), bf16[128,144,128]{2,1,0:T(8,128)(2,1)}, u32[]{:S(2)}, u32[]{:S(2)}) async-start(bf16[128,144,128]{2,1,0:T(8,128)(2,1)} %expert_back.1), calls=%async_computation.3 | async-start | bytes 9437184 | tf_op jit(solution)/shard_map/all_to_all | solution.py:409
  228.8 2.2 combine_weights.1.w_ref
  231.1 60.6 %all-to-all-done.3.msg_ref = bf16[128,144,128]{2,1,0:T(8,128)(2,1)} async-done(((bf16[128,144,128]{2,1,0:T(8,128)(2,1)}), bf16[128,144,128]{2,1,0:T(8,128)(2,1)}, u32[]{:S(2)}, u32[]{:S(2)}) %all-to-all-start.3) | async-done | bytes 4718624 | tf_op jit(solution)/shard_map/all_to_all | solution.py:409
  291.7 5.3 %combine.1 = bf16[128,2048]{1,0:T(8,128)(2,1)} custom-call(bf16[128,144,128]{2,1,0:T(8,128)(2,1)} %all-to-all-done.3.msg_ref, bf16[256,1152]{1,0:T(8,128)(2,1)} %combine_weights.1.w_ref), custom_call_target="tpu_custom_call" | custom-call | flops 5830000128 | bytes 15900000 | tf_op jit(solution)/shard_map/combine/pallas_call | solution.py:392
  (48 shorter events, 12.5 us)
Async XLA Ops:
  0.0 21.0 %collective-permute-start = (bf16[512,256]{1,0:T(8,128)(2,1)}, bf16[512,256]{1,0:T(8,128)(2,1)S(1)}, u32[]{:S(2)}, u32[]{:S(2)}) collective-permute-start(bf16[512,256]{1,0:T(8,128)(2,1)} %param.17), channel_id=1, source_target_pairs={{0,4},{4,8},{8,12},{12,0},{16,20},{20,24},{24,28},{28,16},{32,36},... | collective-permute-start | bytes 786440 | tf_op jit(solution)/shard_map/ppermute | solution.py:438
  1.0 22.5 %collective-permute-start.2 = (bf16[512,256]{1,0:T(8,128)(2,1)}, bf16[512,256]{1,0:T(8,128)(2,1)S(1)}, u32[]{:S(2)}, u32[]{:S(2)}) collective-permute-start(bf16[512,256]{1,0:T(8,128)(2,1)} %param.17), channel_id=1, source_target_pairs={{0,12},{4,0},{8,4},{12,8},{16,28},{20,16},{24,20},{28,24},{32,44},... | collective-permute-start | bytes 786440 | tf_op jit(solution)/shard_map/ppermute | solution.py:438
  1.5 20.3 %collective-permute-start.1 = (bf16[512,256]{1,0:T(8,128)(2,1)}, bf16[512,256]{1,0:T(8,128)(2,1)}, u32[]{:S(2)}, u32[]{:S(2)}) collective-permute-start(bf16[512,256]{1,0:T(8,128)(2,1)} %param.17), channel_id=1, source_target_pairs={{0,8},{4,12},{8,0},{12,4},{16,24},{20,28},{24,16},{28,20},{32,40},... | collective-permute-start | bytes 786440 | tf_op jit(solution)/shard_map/ppermute | solution.py:438
  7.2 11.4 %copy-start.1 = (bf16[512,256]{1,0:T(8,128)(2,1)S(1)}, bf16[512,256]{1,0:T(8,128)(2,1)}, u32[]{:S(2)}) copy-start(bf16[512,256]{1,0:T(8,128)(2,1)} %param.17) | copy-start | bytes 786436
  7.2 41.5 %all-to-all-start.1 = ((bf16[128,72,128]{2,1,0:T(8,128)(2,1)}), bf16[128,72,128]{2,1,0:T(8,128)(2,1)S(1)}, u32[]{:S(2)}, u32[]{:S(2)}) async-start(bf16[128,72,128]{2,1,0:T(8,128)(2,1)} %get-tuple-element.47), calls=%async_computation.1 | async-start | bytes 4718592 | tf_op jit(solution)/shard_map/all_to_all | solution.py:409
  24.9 61.7 %collective-permute-start.3 = (bf16[2,1280,256]{2,1,0:T(8,128)(2,1)}, bf16[2,1280,256]{2,1,0:T(8,128)(2,1)}, u32[]{:S(2)}, u32[]{:S(2)}) collective-permute-start(bf16[2,1280,256]{2,1,0:T(8,128)(2,1)} %constant_dynamic-update-slice_fusion.refs_0_), channel_id=1, source_target_pairs={{0,1},{1,2},{2,3},{3,0},{64,67},{65,64},{66,65},{67,66},{4,5},{5,6... | collective-permute-start | bytes 3932168 | tf_op jit(solution)/shard_map/ppermute | solution.py:460
  26.4 60.3 %collective-permute-start.4 = (bf16[1,1280,256]{2,1,0:T(8,128)(2,1)S(1)}, bf16[1,1280,256]{2,1,0:T(8,128)(2,1)}, u32[]{:S(2)}, u32[]{:S(2)}) collective-permute-start(bf16[1,1280,256]{2,1,0:T(8,128)(2,1)S(1)} %constant_dynamic-slice_fusion), channel_id=1, source_target_pairs={{0,2},{1,3},{2,0},{3,1},{4,6},{5,7},{6,4},{7,5},{8,10},{9,11},{10,... | collective-permute-start | bytes 1966088 | tf_op jit(solution)/shard_map/ppermute | solution.py:461
  44.4 15.1 %collective-permute-start.5 = (bf16[512,512]{1,0:T(8,128)(2,1)}, bf16[512,512]{1,0:T(8,128)(2,1)S(1)}, u32[]{:S(2)}, u32[]{:S(2)}) collective-permute-start(bf16[512,512]{1,0:T(8,128)(2,1)} %bitcast.26), channel_id=1, source_target_pairs={{0,4},{4,8},{8,12},{12,0},{16,20},{20,24},{24,28},{28,16},{32,36},... | collective-permute-start | bytes 1572872 | tf_op jit(solution)/shard_map/ppermute | solution.py:438
  45.4 28.8 %collective-permute-start.6 = (bf16[512,512]{1,0:T(8,128)(2,1)}, bf16[512,512]{1,0:T(8,128)(2,1)}, u32[]{:S(2)}, u32[]{:S(2)}) collective-permute-start(bf16[512,512]{1,0:T(8,128)(2,1)} %bitcast.25), channel_id=1, source_target_pairs={{0,8},{4,12},{8,0},{12,4},{16,24},{20,28},{24,16},{28,20},{32,40},... | collective-permute-start | bytes 1572872 | tf_op jit(solution)/shard_map/ppermute | solution.py:438
  45.9 30.4 %collective-permute-start.7 = (bf16[512,512]{1,0:T(8,128)(2,1)}, bf16[512,512]{1,0:T(8,128)(2,1)}, u32[]{:S(2)}, u32[]{:S(2)}) collective-permute-start(bf16[512,512]{1,0:T(8,128)(2,1)} %bitcast.24), channel_id=1, source_target_pairs={{0,12},{4,0},{8,4},{12,8},{16,28},{20,16},{24,20},{28,24},{32,44},... | collective-permute-start | bytes 1572872 | tf_op jit(solution)/shard_map/ppermute | solution.py:438
  48.7 1.4 copy-start
  50.1 80.2 %all-to-all-start.2 = ((bf16[128,72,128]{2,1,0:T(8,128)(2,1)}), bf16[128,72,128]{2,1,0:T(8,128)(2,1)}, u32[]{:S(2)}, u32[]{:S(2)}) async-start(bf16[128,72,128]{2,1,0:T(8,128)(2,1)} %get-tuple-element.48), calls=%async_computation.2 | async-start | bytes 4718592 | tf_op jit(solution)/shard_map/all_to_all | solution.py:409
  59.5 27.6 %copy-start.4 = (bf16[512,512]{1,0:T(8,128)(2,1)}, bf16[512,512]{1,0:T(8,128)(2,1)S(1)}, u32[]{:S(2)}) copy-start(bf16[512,512]{1,0:T(8,128)(2,1)S(1)} %collective-permute-done.5.x1) | copy-start | bytes 1572868
  86.6 11.4 %collective-permute-start.11 = (bf16[2,1280,256]{2,1,0:T(8,128)(2,1)}, bf16[2,1280,256]{2,1,0:T(8,128)(2,1)S(1)}, u32[]{:S(2)}, u32[]{:S(2)}) collective-permute-start(bf16[2,1280,256]{2,1,0:T(8,128)(2,1)} %collective-permute-done.3.refs_1_), channel_id=1, source_target_pairs={{0,64},{64,0},{1,65},{65,1},{2,66},{66,2},{3,67},{67,3},{4,68},{68... | collective-permute-start | bytes 3932168 | tf_op jit(solution)/shard_map/ppermute | solution.py:480
  86.6 11.4 %collective-permute-start.12 = (bf16[1,1280,256]{2,1,0:T(8,128)(2,1)}, bf16[1,1280,256]{2,1,0:T(8,128)(2,1)S(1)}, u32[]{:S(2)}, u32[]{:S(2)}) collective-permute-start(bf16[1,1280,256]{2,1,0:T(8,128)(2,1)} %collective-permute-done.4.refs_2_), channel_id=1, source_target_pairs={{0,64},{64,0},{1,65},{65,1},{2,66},{66,2},{3,67},{67,3},{4,68},{68... | collective-permute-start | bytes 1966088 | tf_op jit(solution)/shard_map/ppermute | solution.py:480
  92.7 15.2 %collective-permute-start.8 = (bf16[5,128,256]{2,1,0:T(8,128)(2,1)}, bf16[5,128,256]{2,1,0:T(8,128)(2,1)S(1)}, u32[]{:S(2)}, u32[]{:S(2)}) collective-permute-start(bf16[5,128,256]{2,1,0:T(8,128)(2,1)} %get-tuple-element.40), channel_id=1, source_target_pairs={{0,16},{4,20},{8,24},{12,28},{16,32},{20,36},{24,40},{28,44},{32,4... | collective-permute-start | bytes 983048 | tf_op jit(solution)/shard_map/ppermute | solution.py:442
  94.2 21.2 %collective-permute-start.9 = (bf16[5,128,256]{2,1,0:T(8,128)(2,1)}, bf16[5,128,256]{2,1,0:T(8,128)(2,1)S(1)}, u32[]{:S(2)}, u32[]{:S(2)}) collective-permute-start(bf16[5,128,256]{2,1,0:T(8,128)(2,1)} %get-tuple-element.41), channel_id=1, source_target_pairs={{0,32},{4,36},{8,40},{12,44},{16,48},{20,52},{24,56},{28,60},{32,0... | collective-permute-start | bytes 983048 | tf_op jit(solution)/shard_map/ppermute | solution.py:442
  97.1 18.2 %collective-permute-start.10 = (bf16[5,128,256]{2,1,0:T(8,128)(2,1)}, bf16[5,128,256]{2,1,0:T(8,128)(2,1)S(1)}, u32[]{:S(2)}, u32[]{:S(2)}) collective-permute-start(bf16[5,128,256]{2,1,0:T(8,128)(2,1)} %get-tuple-element.42), channel_id=1, source_target_pairs={{0,48},{4,52},{8,56},{12,60},{16,0},{20,4},{24,8},{28,12},{32,16},... | collective-permute-start | bytes 983048 | tf_op jit(solution)/shard_map/ppermute | solution.py:442
  98.0 0.8 copy-start.3
  98.9 1.1 copy-start.2
  104.2 15.2 %collective-permute-start.13 = (bf16[3,128,256]{2,1,0:T(8,128)(2,1)}, bf16[3,128,256]{2,1,0:T(8,128)(2,1)S(1)}, u32[]{:S(2)}, u32[]{:S(2)}) collective-permute-start(bf16[3,128,256]{2,1,0:T(8,128)(2,1)} %get-tuple-element.44), channel_id=1, source_target_pairs={{0,16},{4,20},{8,24},{12,28},{16,32},{20,36},{24,40},{28,44},{32,4... | collective-permute-start | bytes 589832 | tf_op jit(solution)/shard_map/ppermute | solution.py:442
  104.8 18.9 %collective-permute-start.14 = (bf16[3,128,256]{2,1,0:T(8,128)(2,1)}, bf16[3,128,256]{2,1,0:T(8,128)(2,1)S(1)}, u32[]{:S(2)}, u32[]{:S(2)}) collective-permute-start(bf16[3,128,256]{2,1,0:T(8,128)(2,1)} %get-tuple-element.45), channel_id=1, source_target_pairs={{0,32},{4,36},{8,40},{12,44},{16,48},{20,52},{24,56},{28,60},{32,0... | collective-permute-start | bytes 589832 | tf_op jit(solution)/shard_map/ppermute | solution.py:442
  107.9 15.8 %copy-start.5 = (bf16[5,128,256]{2,1,0:T(8,128)(2,1)}, bf16[5,128,256]{2,1,0:T(8,128)(2,1)S(1)}, u32[]{:S(2)}) copy-start(bf16[5,128,256]{2,1,0:T(8,128)(2,1)S(1)} %collective-permute-done.8.m1) | copy-start | bytes 983044
  107.9 15.8 %collective-permute-start.15 = (bf16[3,128,256]{2,1,0:T(8,128)(2,1)}, bf16[3,128,256]{2,1,0:T(8,128)(2,1)S(1)}, u32[]{:S(2)}, u32[]{:S(2)}) collective-permute-start(bf16[3,128,256]{2,1,0:T(8,128)(2,1)} %get-tuple-element.46), channel_id=1, source_target_pairs={{0,48},{4,52},{8,56},{12,60},{16,0},{20,4},{24,8},{28,12},{32,16},... | collective-permute-start | bytes 589832 | tf_op jit(solution)/shard_map/ppermute | solution.py:442
  115.3 8.4 %copy-start.6 = (bf16[5,128,256]{2,1,0:T(8,128)(2,1)}, bf16[5,128,256]{2,1,0:T(8,128)(2,1)S(1)}, u32[]{:S(2)}) copy-start(bf16[5,128,256]{2,1,0:T(8,128)(2,1)S(1)} %collective-permute-done.9.m2) | copy-start | bytes 983044
  115.3 8.4 %copy-start.7 = (bf16[5,128,256]{2,1,0:T(8,128)(2,1)}, bf16[5,128,256]{2,1,0:T(8,128)(2,1)S(1)}, u32[]{:S(2)}) copy-start(bf16[5,128,256]{2,1,0:T(8,128)(2,1)S(1)} %collective-permute-done.10.m3) | copy-start | bytes 983044
  119.4 4.3 %copy-start.8 = (bf16[3,128,256]{2,1,0:T(8,128)(2,1)}, bf16[3,128,256]{2,1,0:T(8,128)(2,1)S(1)}, u32[]{:S(2)}) copy-start(bf16[3,128,256]{2,1,0:T(8,128)(2,1)S(1)} %collective-permute-done.13.o1) | copy-start | bytes 589828
  123.7 0.7 copy-start.9
  123.7 0.7 copy-start.10
  130.3 70.5 %all-to-all-start = ((bf16[128,144,128]{2,1,0:T(8,128)(2,1)}), bf16[128,144,128]{2,1,0:T(8,128)(2,1)}, u32[]{:S(2)}, u32[]{:S(2)}) async-start(bf16[128,144,128]{2,1,0:T(8,128)(2,1)} %sum_pack.1), calls=%async_computation | async-start | bytes 9437184 | tf_op jit(solution)/shard_map/all_to_all | solution.py:409
  221.5 70.2 %all-to-all-start.3 = ((bf16[128,144,128]{2,1,0:T(8,128)(2,1)}), bf16[128,144,128]{2,1,0:T(8,128)(2,1)}, u32[]{:S(2)}, u32[]{:S(2)}) async-start(bf16[128,144,128]{2,1,0:T(8,128)(2,1)} %expert_back.1), calls=%async_computation.3 | async-start | bytes 9437184 | tf_op jit(solution)/shard_map/all_to_all | solution.py:409

commit v4 on v3

--- a/solution.py
+++ b/solution.py
@@ -381,11 +381,14 @@
     scr[...] = msg_ref[:, 64:72, :].astype(F32).reshape(NE * 8, 128)
     w_main = w_ref[:, : NE * 8]
     w_last = w_ref[:, NE * 8 :]
-    for jj in range(8):
-        piece = msg_ref[:, jj * 8 : (jj + 1) * 8, :].reshape(NE * 8, 128)
-        ninth = scr[pl.ds(jj, NE, stride=8), :].astype(BF)
+    for jj in range(0, 8, 2):
+        pair = range(jj, jj + 2)
+        piece = jnp.concatenate(
+            [msg_ref[:, q * 8 : (q + 1) * 8, :].reshape(NE * 8, 128) for q in pair], axis=1
+        )
+        ninth = jnp.concatenate([scr[pl.ds(q, NE, stride=8), :].astype(BF) for q in pair], axis=1)
         both = dot_nn(w_main, piece) + dot_nn(w_last, ninth)
-        out_ref[:, jj * 128 : (jj + 1) * 128] = (both[:TOK] + both[TOK:]).astype(BF)
+        out_ref[:, jj * 128 : (jj + 2) * 128] = (both[:TOK] + both[TOK:]).astype(BF)
 
 
 def combine(msg, weights):

time: 298 us -> 297 us (level)
  no operation moved by 1% of the time
where the time goes in v4:
time: 297 us; the launch traced here: 296 us
  waiting for transfers between devices  158 us (53%)
  Pallas kernels  75.8 us (26%)
  starting transfers between devices  51 us (17%)
  local copies, waits for them, and re-layouts  10.8 us (4%)
    all_to_all x4, waiting for transfers between devices, exchange(): lax.all_to_all(x, axis, split_axis=0, concat_axis=0, tiled=True, axis_ind...  113 us
    all_to_all x4, starting transfers between devices, exchange(): lax.all_to_all(x, axis, split_axis=0, concat_axis=0, tiled=True, axis_ind...  35.8 us
    pallas_call x1, Pallas kernels, expert_back(): pl.pallas_call(expert_kernel, grid=(steps,), in_specs=[pl.BlockSpec((CHUN...  20.7 us
    ppermute x6, waiting for transfers between devices, ahead_z(): return lax.ppermute(x, 'row', hops)  17.7 us
    ppermute x6, waiting for transfers between devices, ahead_y(): return lax.ppermute(x, 'row', hops)  16.8 us
    pallas_call x1, Pallas kernels, attention(): pl.pallas_call(attention_kernel, grid_spec=pltpu.PrefetchScalarGridSpec(n...  15.9 us
    pallas_call x1, Pallas kernels, gate_factors(): pl.pallas_call(gate_up_kernel, grid=(steps,), in_specs=[pl.BlockSpec((CHU...  12.7 us
    ppermute x1, waiting for transfers between devices, body(): lax.ppermute(lax.dynamic_slice_in_dim(w_own, section, 1, 0), 'col', [(c,...  10.3 us
  transfers between devices with their start and end apart: 20, of which 10 were waited for; matrix products, arithmetic and copies ran while one was open for 3% of the time, Pallas kernels for 17%

profile of v4, /device:TPU:19, one launch (start us, length us, event | category | flops | bytes accessed | tf_op | source)
XLA Modules:
  0.0 296.0 jit_solution(16077322878883220640)
XLA Ops:
  0.0 1.0 collective-permute-start
  1.5 1.3 collective-permute-start.1
  2.8 4.4 %route_pack.1 = (bf16[1152,128]{1,0:T(8,128)(2,1)}, bf16[128,72,128]{2,1,0:T(8,128)(2,1)}, bf16[128,72,128]{2,1,0:T(8,128)(2,1)}) custom-call(s32[8,128]{1,0:T(8,128)} %bitcast.27, bf16[128,2048]{1,0:T(8,128)(2,1)} %x_ref.1), custom_call_target="tpu_custom_call" | custom-call | flops 5500000256 | bytes 15000000 | tf_op jit(solution)/shard_map/route_pack/pallas_call | solution.py:102
  7.2 11.4 %all-to-all-start.1 = ((bf16[128,72,128]{2,1,0:T(8,128)(2,1)}), bf16[128,72,128]{2,1,0:T(8,128)(2,1)S(1)}, u32[]{:S(2)}, u32[]{:S(2)}) async-start(bf16[128,72,128]{2,1,0:T(8,128)(2,1)} %get-tuple-element.47), calls=%async_computation.1 | async-start | bytes 4718592 | tf_op jit(solution)/shard_map/all_to_all | solution.py:412
  21.8 1.7 constant_dynamic-update-slice_fusion.2
  25.2 1.2 constant_dynamic-slice_fusion
  26.4 2.2 collective-permute-start.4
  28.5 15.9 %attention.1 = (bf16[4,128,512]{2,1,0:T(8,128)(2,1)}, bf16[4,128,512]{2,1,0:T(8,128)(2,1)}, bf16[4,128,512]{2,1,0:T(8,128)(2,1)}, bf16[4,128,512]{2,1,0:T(8,128)(2,1)}) custom-call(s32[4]{0:T(128)} %pad_add_fusion.at_ref, bf16[2048,256]{1,0:T(8,128)(2,1)} %q_ref, bf16[2048,256]{1,0:T(8,128)(2,1)} %g_ref.1, bf16[2048,512]{1,0:T(8,128)(2,1)} %k_ref.1, ...), custom_call_target="tpu_custom_call" | custom-call | flops 17600000000 | bytes 48000000 | tf_op jit(solution)/shard_map/attention/pallas_call | solution.py:196
  46.8 1.9 all-to-all-done.1.msg0
  48.7 1.4 copy-done
  50.1 9.4 %all-to-all-start.2 = ((bf16[128,72,128]{2,1,0:T(8,128)(2,1)}), bf16[128,72,128]{2,1,0:T(8,128)(2,1)}, u32[]{:S(2)}, u32[]{:S(2)}) async-start(bf16[128,72,128]{2,1,0:T(8,128)(2,1)} %get-tuple-element.48), calls=%async_computation.2 | async-start | bytes 4718592 | tf_op jit(solution)/shard_map/all_to_all | solution.py:412
  59.6 14.7 %collective-permute-done.6.x2 = bf16[512,512]{1,0:T(8,128)(2,1)} collective-permute-done((bf16[512,512]{1,0:T(8,128)(2,1)}, bf16[512,512]{1,0:T(8,128)(2,1)}, u32[]{:S(2)}, u32[]{:S(2)}) %collective-permute-start.6) | collective-permute-done | bytes 524320 | tf_op jit(solution)/shard_map/ppermute | solution.py:441
  74.2 2.1 collective-permute-done.7.x3
  76.3 10.3 %collective-permute-done.4.refs_2_ = bf16[1,1280,256]{2,1,0:T(8,128)(2,1)} collective-permute-done((bf16[1,1280,256]{2,1,0:T(8,128)(2,1)S(1)}, bf16[1,1280,256]{2,1,0:T(8,128)(2,1)}, u32[]{:S(2)}, u32[]{:S(2)}) %collective-permute-start.4) | collective-permute-done | bytes 655392 | tf_op jit(solution)/shard_map/ppermute | solution.py:464
  87.1 5.6 %project.2 = (bf16[5,128,256]{2,1,0:T(8,128)(2,1)}, bf16[5,128,256]{2,1,0:T(8,128)(2,1)}, bf16[5,128,256]{2,1,0:T(8,128)(2,1)}, bf16[5,128,256]{2,1,0:T(8,128)(2,1)}) custom-call(s32[4]{0:T(128)} %pad_add_fusion.at_ref, bf16[512,512]{1,0:T(8,128)(2,1)} %bitcast.30, bf16[512,512]{1,0:T(8,128)(2,1)} %copy-done.4, bf16[512,512]{1,0:T(8,128)(2,1)} %collective-permute-done.6.x2, ...), custom_call_target="tpu_custom_call" | custom-call | flops 3300000000 | bytes 9000000 | tf_op jit(solution)/shard_map/project/pallas_call | solution.py:241
  92.7 1.5 collective-permute-start.8
  94.2 2.9 collective-permute-start.9
  98.9 1.1 copy-done.2
  99.9 4.3 %project.3 = (bf16[3,128,256]{2,1,0:T(8,128)(2,1)}, bf16[3,128,256]{2,1,0:T(8,128)(2,1)}, bf16[3,128,256]{2,1,0:T(8,128)(2,1)}, bf16[3,128,256]{2,1,0:T(8,128)(2,1)}) custom-call(s32[4]{0:T(128)} %pad_add_fusion.at_ref, bf16[512,512]{1,0:T(8,128)(2,1)} %bitcast.31, bf16[512,512]{1,0:T(8,128)(2,1)} %copy-done.4, bf16[512,512]{1,0:T(8,128)(2,1)} %collective-permute-done.6.x2, ...), custom_call_target="tpu_custom_call" | custom-call | flops 1980000000 | bytes 5399999 | tf_op jit(solution)/shard_map/project/pallas_call | solution.py:241
  105.4 2.5 collective-permute-done.8.m1
  108.5 6.8 %collective-permute-done.9.m2 = bf16[5,128,256]{2,1,0:T(8,128)(2,1)S(1)} collective-permute-done((bf16[5,128,256]{2,1,0:T(8,128)(2,1)}, bf16[5,128,256]{2,1,0:T(8,128)(2,1)S(1)}, u32[]{:S(2)}, u32[]{:S(2)}) %collective-permute-start.9) | collective-permute-done | bytes 327712 | tf_op jit(solution)/shard_map/ppermute | solution.py:445
  115.3 4.1 %collective-permute-done.13.o1 = bf16[3,128,256]{2,1,0:T(8,128)(2,1)S(1)} collective-permute-done((bf16[3,128,256]{2,1,0:T(8,128)(2,1)}, bf16[3,128,256]{2,1,0:T(8,128)(2,1)S(1)}, u32[]{:S(2)}, u32[]{:S(2)}) %collective-permute-start.13) | collective-permute-done | bytes 196640 | tf_op jit(solution)/shard_map/ppermute | solution.py:445
  119.4 4.3 %collective-permute-done.14.o2 = bf16[3,128,256]{2,1,0:T(8,128)(2,1)S(1)} collective-permute-done((bf16[3,128,256]{2,1,0:T(8,128)(2,1)}, bf16[3,128,256]{2,1,0:T(8,128)(2,1)S(1)}, u32[]{:S(2)}, u32[]{:S(2)}) %collective-permute-start.14) | collective-permute-done | bytes 196640 | tf_op jit(solution)/shard_map/ppermute | solution.py:445
  124.5 5.8 %sum_pack.1 = bf16[128,144,128]{2,1,0:T(8,128)(2,1)} custom-call(s32[4]{0:T(128)} %pad_add_fusion.at_ref, bf16[5,128,256]{2,1,0:T(8,128)(2,1)} %get-tuple-element.39.m0, bf16[5,128,256]{2,1,0:T(8,128)(2,1)} %copy-done.5, bf16[5,128,256]{2,1,0:T(8,128)(2,1)} %copy-done.6, bf16[5,128,256]{2,1,0:T(8,128)(2,1)} %copy-done.7, ...), custom_call_target="tpu_custom_call" | custom-call | flops 4400000000 | bytes 12000000 | tf_op jit(solution)/shard_map/sum_pack/pallas_call | solution.py:280
  130.3 7.6 %all-to-all-start = ((bf16[128,144,128]{2,1,0:T(8,128)(2,1)}), bf16[128,144,128]{2,1,0:T(8,128)(2,1)}, u32[]{:S(2)}, u32[]{:S(2)}) async-start(bf16[128,144,128]{2,1,0:T(8,128)(2,1)} %sum_pack.1), calls=%async_computation | async-start | bytes 9437184 | tf_op jit(solution)/shard_map/all_to_all | solution.py:412
  138.0 12.7 %gate_factors.1.fac_ref = bf16[1152,1536]{1,0:T(8,128)(2,1)} custom-call(bf16[128,72,128]{2,1,0:T(8,128)(2,1)} %copy-done, bf16[128,72,128]{2,1,0:T(8,128)(2,1)} %all-to-all-done.2.msg1, bf16[2048,1536]{1,0:T(8,128)(2,1)} %bitcast.21), custom_call_target="tpu_custom_call" | custom-call | flops 13749999616 | bytes 37500000 | tf_op jit(solution)/shard_map/gate_factors/pallas_call | solution.py:326
  150.6 50.2 %all-to-all-done.msg0.msg1 = bf16[128,144,128]{2,1,0:T(8,128)(2,1)} async-done(((bf16[128,144,128]{2,1,0:T(8,128)(2,1)}), bf16[128,144,128]{2,1,0:T(8,128)(2,1)}, u32[]{:S(2)}, u32[]{:S(2)}) %all-to-all-start) | async-done | bytes 4718624 | tf_op jit(solution)/shard_map/all_to_all | solution.py:412
  200.8 20.7 %expert_back.1 = bf16[128,144,128]{2,1,0:T(8,128)(2,1)} custom-call(bf16[128,144,128]{2,1,0:T(8,128)(2,1)} %all-to-all-done.msg0.msg1, bf16[128,144,128]{2,1,0:T(8,128)(2,1)} %all-to-all-done.msg0.msg1, bf16[1152,1536]{1,0:T(8,128)(2,1)} %gate_factors.1.fac_ref, bf16[768,2048]{1,0:T(8,128)(2,1)} %bitcast.23, bf16[2048,1536]{1,0:T(8,128)(2,1)} %bitcast.22), custom_call_target="tpu_custom_call" | custom-call | flops 22000001024 | bytes 60000000 | tf_op jit(solution)/shard_map/expert_back/pallas_call | solution.py:361
  221.5 7.3 %all-to-all-start.3 = ((bf16[128,144,128]{2,1,0:T(8,128)(2,1)}), bf16[128,144,128]{2,1,0:T(8,128)(2,1)}, u32[]{:S(2)}, u32[]{:S(2)}) async-start(bf16[128,144,128]{2,1,0:T(8,128)(2,1)} %expert_back.1), calls=%async_computation.3 | async-start | bytes 9437184 | tf_op jit(solution)/shard_map/all_to_all | solution.py:412
  228.8 2.2 combine_weights.1.w_ref
  231.1 60.6 %all-to-all-done.3.msg_ref = bf16[128,144,128]{2,1,0:T(8,128)(2,1)} async-done(((bf16[128,144,128]{2,1,0:T(8,128)(2,1)}), bf16[128,144,128]{2,1,0:T(8,128)(2,1)}, u32[]{:S(2)}, u32[]{:S(2)}) %all-to-all-start.3) | async-done | bytes 4718624 | tf_op jit(solution)/shard_map/all_to_all | solution.py:412
  291.7 4.3 %combine.1 = bf16[128,2048]{1,0:T(8,128)(2,1)} custom-call(bf16[128,144,128]{2,1,0:T(8,128)(2,1)} %all-to-all-done.3.msg_ref, bf16[256,1152]{1,0:T(8,128)(2,1)} %combine_weights.1.w_ref), custom_call_target="tpu_custom_call" | custom-call | flops 5830000128 | bytes 15900000 | tf_op jit(solution)/shard_map/combine/pallas_call | solution.py:395
  (48 shorter events, 12.5 us)
Async XLA Ops:
  0.0 21.0 %collective-permute-start = (bf16[512,256]{1,0:T(8,128)(2,1)}, bf16[512,256]{1,0:T(8,128)(2,1)S(1)}, u32[]{:S(2)}, u32[]{:S(2)}) collective-permute-start(bf16[512,256]{1,0:T(8,128)(2,1)} %param.17), channel_id=1, source_target_pairs={{0,4},{4,8},{8,12},{12,0},{16,20},{20,24},{24,28},{28,16},{32,36},... | collective-permute-start | bytes 786440 | tf_op jit(solution)/shard_map/ppermute | solution.py:441
  1.0 22.5 %collective-permute-start.2 = (bf16[512,256]{1,0:T(8,128)(2,1)}, bf16[512,256]{1,0:T(8,128)(2,1)S(1)}, u32[]{:S(2)}, u32[]{:S(2)}) collective-permute-start(bf16[512,256]{1,0:T(8,128)(2,1)} %param.17), channel_id=1, source_target_pairs={{0,12},{4,0},{8,4},{12,8},{16,28},{20,16},{24,20},{28,24},{32,44},... | collective-permute-start | bytes 786440 | tf_op jit(solution)/shard_map/ppermute | solution.py:441
  1.5 20.3 %collective-permute-start.1 = (bf16[512,256]{1,0:T(8,128)(2,1)}, bf16[512,256]{1,0:T(8,128)(2,1)}, u32[]{:S(2)}, u32[]{:S(2)}) collective-permute-start(bf16[512,256]{1,0:T(8,128)(2,1)} %param.17), channel_id=1, source_target_pairs={{0,8},{4,12},{8,0},{12,4},{16,24},{20,28},{24,16},{28,20},{32,40},... | collective-permute-start | bytes 786440 | tf_op jit(solution)/shard_map/ppermute | solution.py:441
  7.2 11.4 %copy-start.1 = (bf16[512,256]{1,0:T(8,128)(2,1)S(1)}, bf16[512,256]{1,0:T(8,128)(2,1)}, u32[]{:S(2)}) copy-start(bf16[512,256]{1,0:T(8,128)(2,1)} %param.17) | copy-start | bytes 786436
  7.2 41.5 %all-to-all-start.1 = ((bf16[128,72,128]{2,1,0:T(8,128)(2,1)}), bf16[128,72,128]{2,1,0:T(8,128)(2,1)S(1)}, u32[]{:S(2)}, u32[]{:S(2)}) async-start(bf16[128,72,128]{2,1,0:T(8,128)(2,1)} %get-tuple-element.47), calls=%async_computation.1 | async-start | bytes 4718592 | tf_op jit(solution)/shard_map/all_to_all | solution.py:412
  24.9 61.7 %collective-permute-start.3 = (bf16[2,1280,256]{2,1,0:T(8,128)(2,1)}, bf16[2,1280,256]{2,1,0:T(8,128)(2,1)}, u32[]{:S(2)}, u32[]{:S(2)}) collective-permute-start(bf16[2,1280,256]{2,1,0:T(8,128)(2,1)} %constant_dynamic-update-slice_fusion.refs_0_), channel_id=1, source_target_pairs={{0,1},{1,2},{2,3},{3,0},{64,67},{65,64},{66,65},{67,66},{4,5},{5,6... | collective-permute-start | bytes 3932168 | tf_op jit(solution)/shard_map/ppermute | solution.py:463
  26.4 60.3 %collective-permute-start.4 = (bf16[1,1280,256]{2,1,0:T(8,128)(2,1)S(1)}, bf16[1,1280,256]{2,1,0:T(8,128)(2,1)}, u32[]{:S(2)}, u32[]{:S(2)}) collective-permute-start(bf16[1,1280,256]{2,1,0:T(8,128)(2,1)S(1)} %constant_dynamic-slice_fusion), channel_id=1, source_target_pairs={{0,2},{1,3},{2,0},{3,1},{4,6},{5,7},{6,4},{7,5},{8,10},{9,11},{10,... | collective-permute-start | bytes 1966088 | tf_op jit(solution)/shard_map/ppermute | solution.py:464
  44.4 15.1 %collective-permute-start.5 = (bf16[512,512]{1,0:T(8,128)(2,1)}, bf16[512,512]{1,0:T(8,128)(2,1)S(1)}, u32[]{:S(2)}, u32[]{:S(2)}) collective-permute-start(bf16[512,512]{1,0:T(8,128)(2,1)} %bitcast.26), channel_id=1, source_target_pairs={{0,4},{4,8},{8,12},{12,0},{16,20},{20,24},{24,28},{28,16},{32,36},... | collective-permute-start | bytes 1572872 | tf_op jit(solution)/shard_map/ppermute | solution.py:441
  45.4 28.8 %collective-permute-start.6 = (bf16[512,512]{1,0:T(8,128)(2,1)}, bf16[512,512]{1,0:T(8,128)(2,1)}, u32[]{:S(2)}, u32[]{:S(2)}) collective-permute-start(bf16[512,512]{1,0:T(8,128)(2,1)} %bitcast.25), channel_id=1, source_target_pairs={{0,8},{4,12},{8,0},{12,4},{16,24},{20,28},{24,16},{28,20},{32,40},... | collective-permute-start | bytes 1572872 | tf_op jit(solution)/shard_map/ppermute | solution.py:441
  45.9 30.4 %collective-permute-start.7 = (bf16[512,512]{1,0:T(8,128)(2,1)}, bf16[512,512]{1,0:T(8,128)(2,1)}, u32[]{:S(2)}, u32[]{:S(2)}) collective-permute-start(bf16[512,512]{1,0:T(8,128)(2,1)} %bitcast.24), channel_id=1, source_target_pairs={{0,12},{4,0},{8,4},{12,8},{16,28},{20,16},{24,20},{28,24},{32,44},... | collective-permute-start | bytes 1572872 | tf_op jit(solution)/shard_map/ppermute | solution.py:441
  48.7 1.4 copy-start
  50.1 80.2 %all-to-all-start.2 = ((bf16[128,72,128]{2,1,0:T(8,128)(2,1)}), bf16[128,72,128]{2,1,0:T(8,128)(2,1)}, u32[]{:S(2)}, u32[]{:S(2)}) async-start(bf16[128,72,128]{2,1,0:T(8,128)(2,1)} %get-tuple-element.48), calls=%async_computation.2 | async-start | bytes 4718592 | tf_op jit(solution)/shard_map/all_to_all | solution.py:412
  59.5 27.6 %copy-start.4 = (bf16[512,512]{1,0:T(8,128)(2,1)}, bf16[512,512]{1,0:T(8,128)(2,1)S(1)}, u32[]{:S(2)}) copy-start(bf16[512,512]{1,0:T(8,128)(2,1)S(1)} %collective-permute-done.5.x1) | copy-start | bytes 1572868
  86.6 11.4 %collective-permute-start.11 = (bf16[2,1280,256]{2,1,0:T(8,128)(2,1)}, bf16[2,1280,256]{2,1,0:T(8,128)(2,1)S(1)}, u32[]{:S(2)}, u32[]{:S(2)}) collective-permute-start(bf16[2,1280,256]{2,1,0:T(8,128)(2,1)} %collective-permute-done.3.refs_1_), channel_id=1, source_target_pairs={{0,64},{64,0},{1,65},{65,1},{2,66},{66,2},{3,67},{67,3},{4,68},{68... | collective-permute-start | bytes 3932168 | tf_op jit(solution)/shard_map/ppermute | solution.py:483
  86.6 11.4 %collective-permute-start.12 = (bf16[1,1280,256]{2,1,0:T(8,128)(2,1)}, bf16[1,1280,256]{2,1,0:T(8,128)(2,1)S(1)}, u32[]{:S(2)}, u32[]{:S(2)}) collective-permute-start(bf16[1,1280,256]{2,1,0:T(8,128)(2,1)} %collective-permute-done.4.refs_2_), channel_id=1, source_target_pairs={{0,64},{64,0},{1,65},{65,1},{2,66},{66,2},{3,67},{67,3},{4,68},{68... | collective-permute-start | bytes 1966088 | tf_op jit(solution)/shard_map/ppermute | solution.py:483
  92.7 15.2 %collective-permute-start.8 = (bf16[5,128,256]{2,1,0:T(8,128)(2,1)}, bf16[5,128,256]{2,1,0:T(8,128)(2,1)S(1)}, u32[]{:S(2)}, u32[]{:S(2)}) collective-permute-start(bf16[5,128,256]{2,1,0:T(8,128)(2,1)} %get-tuple-element.40), channel_id=1, source_target_pairs={{0,16},{4,20},{8,24},{12,28},{16,32},{20,36},{24,40},{28,44},{32,4... | collective-permute-start | bytes 983048 | tf_op jit(solution)/shard_map/ppermute | solution.py:445
  94.2 21.2 %collective-permute-start.9 = (bf16[5,128,256]{2,1,0:T(8,128)(2,1)}, bf16[5,128,256]{2,1,0:T(8,128)(2,1)S(1)}, u32[]{:S(2)}, u32[]{:S(2)}) collective-permute-start(bf16[5,128,256]{2,1,0:T(8,128)(2,1)} %get-tuple-element.41), channel_id=1, source_target_pairs={{0,32},{4,36},{8,40},{12,44},{16,48},{20,52},{24,56},{28,60},{32,0... | collective-permute-start | bytes 983048 | tf_op jit(solution)/shard_map/ppermute | solution.py:445
  97.1 18.2 %collective-permute-start.10 = (bf16[5,128,256]{2,1,0:T(8,128)(2,1)}, bf16[5,128,256]{2,1,0:T(8,128)(2,1)S(1)}, u32[]{:S(2)}, u32[]{:S(2)}) collective-permute-start(bf16[5,128,256]{2,1,0:T(8,128)(2,1)} %get-tuple-element.42), channel_id=1, source_target_pairs={{0,48},{4,52},{8,56},{12,60},{16,0},{20,4},{24,8},{28,12},{32,16},... | collective-permute-start | bytes 983048 | tf_op jit(solution)/shard_map/ppermute | solution.py:445
  98.0 0.8 copy-start.3
  98.9 1.1 copy-start.2
  104.2 15.2 %collective-permute-start.13 = (bf16[3,128,256]{2,1,0:T(8,128)(2,1)}, bf16[3,128,256]{2,1,0:T(8,128)(2,1)S(1)}, u32[]{:S(2)}, u32[]{:S(2)}) collective-permute-start(bf16[3,128,256]{2,1,0:T(8,128)(2,1)} %get-tuple-element.44), channel_id=1, source_target_pairs={{0,16},{4,20},{8,24},{12,28},{16,32},{20,36},{24,40},{28,44},{32,4... | collective-permute-start | bytes 589832 | tf_op jit(solution)/shard_map/ppermute | solution.py:445
  104.8 18.9 %collective-permute-start.14 = (bf16[3,128,256]{2,1,0:T(8,128)(2,1)}, bf16[3,128,256]{2,1,0:T(8,128)(2,1)S(1)}, u32[]{:S(2)}, u32[]{:S(2)}) collective-permute-start(bf16[3,128,256]{2,1,0:T(8,128)(2,1)} %get-tuple-element.45), channel_id=1, source_target_pairs={{0,32},{4,36},{8,40},{12,44},{16,48},{20,52},{24,56},{28,60},{32,0... | collective-permute-start | bytes 589832 | tf_op jit(solution)/shard_map/ppermute | solution.py:445
  107.9 15.8 %copy-start.5 = (bf16[5,128,256]{2,1,0:T(8,128)(2,1)}, bf16[5,128,256]{2,1,0:T(8,128)(2,1)S(1)}, u32[]{:S(2)}) copy-start(bf16[5,128,256]{2,1,0:T(8,128)(2,1)S(1)} %collective-permute-done.8.m1) | copy-start | bytes 983044
  107.9 15.8 %collective-permute-start.15 = (bf16[3,128,256]{2,1,0:T(8,128)(2,1)}, bf16[3,128,256]{2,1,0:T(8,128)(2,1)S(1)}, u32[]{:S(2)}, u32[]{:S(2)}) collective-permute-start(bf16[3,128,256]{2,1,0:T(8,128)(2,1)} %get-tuple-element.46), channel_id=1, source_target_pairs={{0,48},{4,52},{8,56},{12,60},{16,0},{20,4},{24,8},{28,12},{32,16},... | collective-permute-start | bytes 589832 | tf_op jit(solution)/shard_map/ppermute | solution.py:445
  115.3 8.4 %copy-start.6 = (bf16[5,128,256]{2,1,0:T(8,128)(2,1)}, bf16[5,128,256]{2,1,0:T(8,128)(2,1)S(1)}, u32[]{:S(2)}) copy-start(bf16[5,128,256]{2,1,0:T(8,128)(2,1)S(1)} %collective-permute-done.9.m2) | copy-start | bytes 983044
  115.3 8.4 %copy-start.7 = (bf16[5,128,256]{2,1,0:T(8,128)(2,1)}, bf16[5,128,256]{2,1,0:T(8,128)(2,1)S(1)}, u32[]{:S(2)}) copy-start(bf16[5,128,256]{2,1,0:T(8,128)(2,1)S(1)} %collective-permute-done.10.m3) | copy-start | bytes 983044
  119.4 4.3 %copy-start.8 = (bf16[3,128,256]{2,1,0:T(8,128)(2,1)}, bf16[3,128,256]{2,1,0:T(8,128)(2,1)S(1)}, u32[]{:S(2)}) copy-start(bf16[3,128,256]{2,1,0:T(8,128)(2,1)S(1)} %collective-permute-done.13.o1) | copy-start | bytes 589828
  123.7 0.7 copy-start.9
  123.7 0.7 copy-start.10
  130.3 70.5 %all-to-all-start = ((bf16[128,144,128]{2,1,0:T(8,128)(2,1)}), bf16[128,144,128]{2,1,0:T(8,128)(2,1)}, u32[]{:S(2)}, u32[]{:S(2)}) async-start(bf16[128,144,128]{2,1,0:T(8,128)(2,1)} %sum_pack.1), calls=%async_computation | async-start | bytes 9437184 | tf_op jit(solution)/shard_map/all_to_all | solution.py:412
  221.5 70.2 %all-to-all-start.3 = ((bf16[128,144,128]{2,1,0:T(8,128)(2,1)}), bf16[128,144,128]{2,1,0:T(8,128)(2,1)}, u32[]{:S(2)}, u32[]{:S(2)}) async-start(bf16[128,144,128]{2,1,0:T(8,128)(2,1)} %expert_back.1), calls=%async_computation.3 | async-start | bytes 9437184 | tf_op jit(solution)/shard_map/all_to_all | solution.py:412
